TPU v7x, 32 devices: a whole 2x2x4 slice. The times are simulated.
32 devices in a mesh: gx: 4 (over z), gy: 8 (over y, x, core).
Axes of the slice: x: 2, y: 2, z: 4, core: 2. Of those that a mesh axis runs over, the one named last changes fastest.
Arguments:
- positions: float32 [3, 4, 8, 2048], P(None, 'gx', 'gy'), as said below
- velocities: float32 [3, 4, 8, 2048], P(None, 'gx', 'gy'), may hold values from -0.1 to 0.1
- bead_types: int32 [4, 8, 2048], P('gx', 'gy'), may hold values from 0 to 18, as said below
- eps_table: float32 [18, 18], replicated, may hold values from 2 to 5.6
- charges: float32 [18], replicated, may hold values from -1 to 1
- x_list: int32 [4, 8, 512], P('gx', 'gy'), may hold values from 0 to 2047, as said below
- y_list: int32 [4, 8, 512], P('gx', 'gy'), may hold values from 0 to 2047, as said below
- tiles: int32 [4, 8, 2, 112], P('gx', 'gy'), may hold values from 0 to 26, as said below
Outputs:
- new_positions: float32 [3, 4, 8, 2048], P(None, 'gx', 'gy')
- new_velocities: float32 [3, 4, 8, 2048], P(None, 'gx', 'gy')
Inputs may be any that keep to these rules, and one draw needn't show every extreme that they name: `positions`: each column's slots fill a lattice of 8 x 8 x 32 sites of spacing 0.43 nm in the column's frame, one slot a site; slots 128 * c to 128 * c + 127 hold the sites of layers 2c and 2c + 1 in some order, and each bead lies within 0.03 nm of its site in every coordinate. `bead_types`: type 18 marks an empty slot; a column's empty slots are exactly its sites in layers at or above its filled height, a multiple of 2 from 2 to 32; columns (0 or 1, 0 or 1) are full. `x_list`: entry e names the slot at the site with x index e % 2, y index (e // 2) % 8 and layer e // 16. `y_list`: entry e names the slot at the site with x index e % 8, y index (e // 8) % 2 and layer e // 16. Zone clusters 0 to 24 are the own, x-import, y-import and corner clusters in the order of the zone beads; a column's real tiles come first, at most 101 of them, reached by column (0, 0), and every later slot holds the pair (25, 26).
All inputs are finite; a program needn't handle non-finite values.
Results may differ from a plain program's by a relative error of at most 0.0003.
Values sent between devices are 32-bit elements; how exact they have to be, the bound alone decides.
A program may use at most 64 MiB of HBM per device.

v0:
```python
import jax
import jax.numpy as jnp
from jax import lax
from jax.sharding import PartitionSpec as P

SIDE = 8
LAYERS = 32
NTYPES = 18
STEPS = 4


SPACING = 0.43
CUTOFF = 1.1
SIGMA = 0.41
COULOMB = 138.935458 / 15.0
MASS = 72.0
TIME_STEP = 0.02


def from_behind(array, axis, by):
    peers = lax.axis_size(axis)
    return lax.ppermute(array, axis, [(i, (i + by) % peers) for i in range(peers)])


def pair_block(pos_a, pos_b, eps_rows, onehot_b, charge_a, charge_b, same_tile):
    width_c = pos_a.shape[2]
    offsets = []
    for component in range(3):
        offsets.append(pos_a[component][:, :, None] - pos_b[component][:, None, :])
    dist_sq = offsets[0] * offsets[0] + offsets[1] * offsets[1] + offsets[2] * offsets[2]
    diagonal = jnp.eye(width_c, dtype=jnp.float32)
    self_pair = same_tile[:, None, None] * diagonal[None]
    dist_sq = dist_sq + self_pair
    eps_pair = jnp.einsum("kni,knj->kij", eps_rows, onehot_b, precision=lax.Precision.HIGHEST)
    inv_sq = 1.0 / dist_sq
    inv_r = jnp.sqrt(inv_sq)
    sixth_pow = (SIGMA * SIGMA * inv_sq) ** 3
    lennard = 24.0 * eps_pair * (2.0 * sixth_pow * sixth_pow - sixth_pow) * inv_sq
    coulomb = (
        COULOMB * charge_a[:, :, None] * charge_b[:, None, :] * (inv_sq * inv_r - 1.0 / CUTOFF**3)
    )
    cut_ratio = dist_sq / (CUTOFF * CUTOFF)
    switch = jnp.where(cut_ratio < 1.0, (1.0 - cut_ratio) ** 2, 0.0)
    weight = (1.0 - 0.5 * same_tile)[:, None, None] * (1.0 - self_pair)
    scalar = weight * switch * (lennard + coulomb)
    on_a = jnp.stack([jnp.sum(scalar * offsets[component], axis=2) for component in range(3)])
    on_b = -jnp.stack([jnp.sum(scalar * offsets[component], axis=1) for component in range(3)])
    return (on_a, on_b)


def zone_forces(pos_zone, kind_zone, tile_pairs, eps_sym, charges):
    type_range = jnp.arange(NTYPES, dtype=jnp.int32)
    onehot = (kind_zone[:, None, :] == type_range[None, :, None]).astype(jnp.float32)
    eps_rows = jnp.einsum("nm,zmc->znc", eps_sym, onehot, precision=lax.Precision.HIGHEST)
    charge = jnp.einsum("m,zmc->zc", charges, onehot, precision=lax.Precision.HIGHEST)
    blocks = tile_pairs.reshape(2, -1, 16).transpose(1, 0, 2)

    def one_block(summed, block_pair):
        left_ids = block_pair[0]
        right_ids = block_pair[1]
        same_tile = (left_ids == right_ids).astype(jnp.float32)
        on_a, on_b = pair_block(
            pos_zone[:, left_ids],
            pos_zone[:, right_ids],
            eps_rows[left_ids],
            onehot[right_ids],
            charge[left_ids],
            charge[right_ids],
            same_tile,
        )
        summed = summed.at[:, left_ids].add(on_a)
        summed = summed.at[:, right_ids].add(on_b)
        return (summed, None)

    summed, unused = lax.scan(one_block, jnp.zeros_like(pos_zone), blocks)
    return summed


def empty_clusters(cluster):
    depth = jnp.concatenate(
        [jnp.full((cluster,), -1000.0, jnp.float32), jnp.full((cluster,), -3000.0, jnp.float32)]
    )
    plain = jnp.zeros((2 * cluster,), jnp.float32)
    return jnp.stack([plain, plain, depth])


def make_packet(coords, kind_ids, index_list):
    rows = coords[:, index_list]
    rows = jnp.concatenate([rows, kind_ids[index_list].astype(jnp.float32)[None, :]], axis=0)
    return rows


def step_forces(coords, kind_ids, x_index, y_index, tile_pairs, eps_sym, charges):
    column_width = SIDE * SPACING
    cluster = 2 * SIDE * SIDE
    strip_size = 2 * SIDE * LAYERS
    corner_size = 4 * LAYERS
    beads = coords.shape[1]
    shift_x = jnp.array([column_width, 0.0, 0.0], dtype=jnp.float32)[:, None]
    shift_y = jnp.array([0.0, column_width, 0.0], dtype=jnp.float32)[:, None]
    packet_x = make_packet(coords, kind_ids, x_index)
    packet_y = make_packet(coords, kind_ids, y_index)
    got_y = from_behind(packet_y, "gy", -1)
    pos_y = got_y[:3] + shift_y
    corner_block = pos_y.reshape(3, LAYERS, 2, SIDE)[:, :, :, :2].reshape(3, corner_size)
    corner_kind = got_y[3].reshape(LAYERS, 2, SIDE)[:, :, :2].reshape(1, corner_size)
    corner_block = jnp.concatenate([corner_block, corner_kind], axis=0)
    joint = jnp.concatenate([packet_x, corner_block], axis=1)
    got_x = from_behind(joint, "gx", -1)
    pos_x = got_x[:3, :strip_size] + shift_x
    pos_c = got_x[:3, strip_size:] + shift_x
    kinds = (
        got_x[3, :strip_size].astype(jnp.int32),
        got_y[3].astype(jnp.int32),
        got_x[3, strip_size:].astype(jnp.int32),
    )
    kind_x, kind_y, kind_c = kinds
    far_zone = empty_clusters(cluster)
    far_kind = jnp.full((2 * cluster,), NTYPES, jnp.int32)
    pos_zone = jnp.concatenate([coords, pos_x, pos_y, pos_c, far_zone], axis=1).reshape(
        3, -1, cluster
    )
    kind_zone = jnp.concatenate([kind_ids, kind_x, kind_y, kind_c, far_kind]).reshape(-1, cluster)
    forces = zone_forces(pos_zone, kind_zone, tile_pairs, eps_sym, charges).reshape(3, -1)
    f_home = forces[:, :beads]
    f_x = forces[:, beads : beads + strip_size]
    f_y = forces[:, beads + strip_size : beads + 2 * strip_size]
    f_c = forces[:, beads + 2 * strip_size : beads + 2 * strip_size + corner_size]
    back_x = from_behind(jnp.concatenate([f_x, f_c], axis=1), "gx", 1)
    own_x = back_x[:, :strip_size]
    relayed = back_x[:, strip_size:].reshape(3, LAYERS, 2, 2)
    f_y = f_y.reshape(3, LAYERS, 2, SIDE).at[:, :, :, :2].add(relayed).reshape(3, strip_size)
    own_y = from_behind(f_y, "gy", 1)
    return f_home.at[:, x_index].add(own_x).at[:, y_index].add(own_y)


def per_device(positions, velocities, bead_types, eps_table, charges, x_list, y_list, tiles):
    coords = positions.reshape(3, -1)
    speeds = velocities.reshape(3, -1)
    kind_ids = bead_types.reshape(-1)
    x_index = x_list.reshape(-1)
    y_index = y_list.reshape(-1)
    tile_pairs = tiles.reshape(2, -1)
    eps_sym = 0.5 * (eps_table + eps_table.T)
    for turn_index in range(STEPS):
        force = step_forces(coords, kind_ids, x_index, y_index, tile_pairs, eps_sym, charges)
        speeds = speeds + TIME_STEP / MASS * force
        coords = coords + TIME_STEP * speeds
    return (coords.reshape(positions.shape), speeds.reshape(velocities.shape))


def solution(mesh):
    return jax.shard_map(
        per_device,
        mesh=mesh,
        in_specs=(
            P(None, "gx", "gy", None),
            P(None, "gx", "gy", None),
            P("gx", "gy", None),
            P(),
            P(),
            P("gx", "gy", None),
            P("gx", "gy", None),
            P("gx", "gy", None, None),
        ),
        out_specs=(P(None, "gx", "gy", None), P(None, "gx", "gy", None)),
        check_vma=False,
    )
```

profile of v0, /device:TPU:0, one launch (start us, length us, event | category | flops | bytes accessed | tf_op | source)
XLA Modules:
  0.0 476.0 jit_solution(4210816116663311944)
XLA Ops:
  2.1 3.4 gather_fusion.27
  7.1 3.4 collective-permute-start
  11.0 3.1 gather_fusion.25
  16.0 3.7 collective-permute-start.1
  22.0 76.9 %while.56 = (s32[]{:T(128)}, f32[3,27,128]{2,0,1:T(4,128)S(1)}, s32[7,2,16]{2,1,0:T(2,128)S(1)}, f32[3,27,128]{2,0,1:T(4,128)S(1)}, f32[27,18,128]{2,1,0:T(8,128...) while((s32[]{:T(128)}, f32[3,27,128]{2,0,1:T(4,128)S(1)}, ...), condition=%wide.region_9.10_spmd.clone, body=%wide.region_0.9_spmd.clone.sunk | while | flops 68087472 | bytes 1894617 | solution.py:75
  25.6 5.0 %fusion.193 = (f32[16,128]{1,0:T(8,128)S(1)}, f32[16,128]{1,0:T(8,128)S(1)}, f32[16,128]{1,0:T(8,128)S(1)}, f32[16,128]{1,0:T(8,128)S(1)}, f32[16,128]{1,0:T(8,128)S(1)}, /*index=5*/f32[16,128]{1,0:T(8,128)S(1)}) fusion(f32[16,128]{1,0:T(8,128)S(1)} %bitcast.550, f32[16,128]{1,0:T(8,128)S(1)} %bitcast.562, f32[16,128]{1,0:T(8,128)S(1)} %bitcast.552, ...), kind=kOutput, calls=%fused_computation.76.clone.1 | convolution fusion | flops 67883008 | bytes 475264 | tf_op jit(solution)/shard_map/while/body/eval_jaxpr/kni,knj->kij/dot_general | solution.py:34
  36.6 5.0 %fusion.193 = (f32[16,128]{1,0:T(8,128)S(1)}, f32[16,128]{1,0:T(8,128)S(1)}, f32[16,128]{1,0:T(8,128)S(1)}, f32[16,128]{1,0:T(8,128)S(1)}, f32[16,128]{1,0:T(8,128)S(1)}, /*index=5*/f32[16,128]{1,0:T(8,128)S(1)}) fusion(f32[16,128]{1,0:T(8,128)S(1)} %bitcast.550, f32[16,128]{1,0:T(8,128)S(1)} %bitcast.562, f32[16,128]{1,0:T(8,128)S(1)} %bitcast.552, ...), kind=kOutput, calls=%fused_computation.76.clone.1 | convolution fusion | flops 67883008 | bytes 475264 | tf_op jit(solution)/shard_map/while/body/eval_jaxpr/kni,knj->kij/dot_general | solution.py:34
  47.6 5.0 %fusion.193 = (f32[16,128]{1,0:T(8,128)S(1)}, f32[16,128]{1,0:T(8,128)S(1)}, f32[16,128]{1,0:T(8,128)S(1)}, f32[16,128]{1,0:T(8,128)S(1)}, f32[16,128]{1,0:T(8,128)S(1)}, /*index=5*/f32[16,128]{1,0:T(8,128)S(1)}) fusion(f32[16,128]{1,0:T(8,128)S(1)} %bitcast.550, f32[16,128]{1,0:T(8,128)S(1)} %bitcast.562, f32[16,128]{1,0:T(8,128)S(1)} %bitcast.552, ...), kind=kOutput, calls=%fused_computation.76.clone.1 | convolution fusion | flops 67883008 | bytes 475264 | tf_op jit(solution)/shard_map/while/body/eval_jaxpr/kni,knj->kij/dot_general | solution.py:34
  58.6 5.0 %fusion.193 = (f32[16,128]{1,0:T(8,128)S(1)}, f32[16,128]{1,0:T(8,128)S(1)}, f32[16,128]{1,0:T(8,128)S(1)}, f32[16,128]{1,0:T(8,128)S(1)}, f32[16,128]{1,0:T(8,128)S(1)}, /*index=5*/f32[16,128]{1,0:T(8,128)S(1)}) fusion(f32[16,128]{1,0:T(8,128)S(1)} %bitcast.550, f32[16,128]{1,0:T(8,128)S(1)} %bitcast.562, f32[16,128]{1,0:T(8,128)S(1)} %bitcast.552, ...), kind=kOutput, calls=%fused_computation.76.clone.1 | convolution fusion | flops 67883008 | bytes 475264 | tf_op jit(solution)/shard_map/while/body/eval_jaxpr/kni,knj->kij/dot_general | solution.py:34
  69.5 5.0 %fusion.193 = (f32[16,128]{1,0:T(8,128)S(1)}, f32[16,128]{1,0:T(8,128)S(1)}, f32[16,128]{1,0:T(8,128)S(1)}, f32[16,128]{1,0:T(8,128)S(1)}, f32[16,128]{1,0:T(8,128)S(1)}, /*index=5*/f32[16,128]{1,0:T(8,128)S(1)}) fusion(f32[16,128]{1,0:T(8,128)S(1)} %bitcast.550, f32[16,128]{1,0:T(8,128)S(1)} %bitcast.562, f32[16,128]{1,0:T(8,128)S(1)} %bitcast.552, ...), kind=kOutput, calls=%fused_computation.76.clone.1 | convolution fusion | flops 67883008 | bytes 475264 | tf_op jit(solution)/shard_map/while/body/eval_jaxpr/kni,knj->kij/dot_general | solution.py:34
  80.5 5.0 %fusion.193 = (f32[16,128]{1,0:T(8,128)S(1)}, f32[16,128]{1,0:T(8,128)S(1)}, f32[16,128]{1,0:T(8,128)S(1)}, f32[16,128]{1,0:T(8,128)S(1)}, f32[16,128]{1,0:T(8,128)S(1)}, /*index=5*/f32[16,128]{1,0:T(8,128)S(1)}) fusion(f32[16,128]{1,0:T(8,128)S(1)} %bitcast.550, f32[16,128]{1,0:T(8,128)S(1)} %bitcast.562, f32[16,128]{1,0:T(8,128)S(1)} %bitcast.552, ...), kind=kOutput, calls=%fused_computation.76.clone.1 | convolution fusion | flops 67883008 | bytes 475264 | tf_op jit(solution)/shard_map/while/body/eval_jaxpr/kni,knj->kij/dot_general | solution.py:34
  91.5 5.0 %fusion.193 = (f32[16,128]{1,0:T(8,128)S(1)}, f32[16,128]{1,0:T(8,128)S(1)}, f32[16,128]{1,0:T(8,128)S(1)}, f32[16,128]{1,0:T(8,128)S(1)}, f32[16,128]{1,0:T(8,128)S(1)}, /*index=5*/f32[16,128]{1,0:T(8,128)S(1)}) fusion(f32[16,128]{1,0:T(8,128)S(1)} %bitcast.550, f32[16,128]{1,0:T(8,128)S(1)} %bitcast.562, f32[16,128]{1,0:T(8,128)S(1)} %bitcast.552, ...), kind=kOutput, calls=%fused_computation.76.clone.1 | convolution fusion | flops 67883008 | bytes 475264 | tf_op jit(solution)/shard_map/while/body/eval_jaxpr/kni,knj->kij/dot_general | solution.py:34
  105.8 2.0 copy.162
  111.0 2.0 copy.122
  114.8 4.1 scatter_fusion.8
  118.9 1.8 collective-permute-done.3
  120.7 4.3 scatter_custom_fusion.9
  126.3 2.3 gather_fusion.29
  129.5 2.3 gather_fusion.28
  134.2 3.1 collective-permute-start.5
  139.6 76.9 %while.57 = (s32[]{:T(128)}, f32[3,27,128]{2,0,1:T(4,128)S(1)}, s32[7,2,16]{2,1,0:T(2,128)S(1)}, f32[3,27,128]{2,0,1:T(4,128)S(1)}, f32[27,18,128]{2,1,0:T(8,128...) while((s32[]{:T(128)}, f32[3,27,128]{2,0,1:T(4,128)S(1)}, ...), condition=%wide.region_21.22_spmd.clone, body=%wide.region_12.21_spmd.clone.sunk | while | flops 68087472 | bytes 1894617 | solution.py:75
  143.2 5.0 %fusion.202 = (f32[16,128]{1,0:T(8,128)S(1)}, f32[16,128]{1,0:T(8,128)S(1)}, f32[16,128]{1,0:T(8,128)S(1)}, f32[16,128]{1,0:T(8,128)S(1)}, f32[16,128]{1,0:T(8,128)S(1)}, /*index=5*/f32[16,128]{1,0:T(8,128)S(1)}) fusion(f32[16,128]{1,0:T(8,128)S(1)} %bitcast.553, f32[16,128]{1,0:T(8,128)S(1)} %bitcast.565, f32[16,128]{1,0:T(8,128)S(1)} %bitcast.555, ...), kind=kOutput, calls=%fused_computation.122.clone.1 | convolution fusion | flops 67883008 | bytes 475264 | tf_op jit(solution)/shard_map/while/body/eval_jaxpr/kni,knj->kij/dot_general | solution.py:34
  154.2 5.0 %fusion.202 = (f32[16,128]{1,0:T(8,128)S(1)}, f32[16,128]{1,0:T(8,128)S(1)}, f32[16,128]{1,0:T(8,128)S(1)}, f32[16,128]{1,0:T(8,128)S(1)}, f32[16,128]{1,0:T(8,128)S(1)}, /*index=5*/f32[16,128]{1,0:T(8,128)S(1)}) fusion(f32[16,128]{1,0:T(8,128)S(1)} %bitcast.553, f32[16,128]{1,0:T(8,128)S(1)} %bitcast.565, f32[16,128]{1,0:T(8,128)S(1)} %bitcast.555, ...), kind=kOutput, calls=%fused_computation.122.clone.1 | convolution fusion | flops 67883008 | bytes 475264 | tf_op jit(solution)/shard_map/while/body/eval_jaxpr/kni,knj->kij/dot_general | solution.py:34
  165.2 5.0 %fusion.202 = (f32[16,128]{1,0:T(8,128)S(1)}, f32[16,128]{1,0:T(8,128)S(1)}, f32[16,128]{1,0:T(8,128)S(1)}, f32[16,128]{1,0:T(8,128)S(1)}, f32[16,128]{1,0:T(8,128)S(1)}, /*index=5*/f32[16,128]{1,0:T(8,128)S(1)}) fusion(f32[16,128]{1,0:T(8,128)S(1)} %bitcast.553, f32[16,128]{1,0:T(8,128)S(1)} %bitcast.565, f32[16,128]{1,0:T(8,128)S(1)} %bitcast.555, ...), kind=kOutput, calls=%fused_computation.122.clone.1 | convolution fusion | flops 67883008 | bytes 475264 | tf_op jit(solution)/shard_map/while/body/eval_jaxpr/kni,knj->kij/dot_general | solution.py:34
  176.2 5.0 %fusion.202 = (f32[16,128]{1,0:T(8,128)S(1)}, f32[16,128]{1,0:T(8,128)S(1)}, f32[16,128]{1,0:T(8,128)S(1)}, f32[16,128]{1,0:T(8,128)S(1)}, f32[16,128]{1,0:T(8,128)S(1)}, /*index=5*/f32[16,128]{1,0:T(8,128)S(1)}) fusion(f32[16,128]{1,0:T(8,128)S(1)} %bitcast.553, f32[16,128]{1,0:T(8,128)S(1)} %bitcast.565, f32[16,128]{1,0:T(8,128)S(1)} %bitcast.555, ...), kind=kOutput, calls=%fused_computation.122.clone.1 | convolution fusion | flops 67883008 | bytes 475264 | tf_op jit(solution)/shard_map/while/body/eval_jaxpr/kni,knj->kij/dot_general | solution.py:34
  187.2 5.0 %fusion.202 = (f32[16,128]{1,0:T(8,128)S(1)}, f32[16,128]{1,0:T(8,128)S(1)}, f32[16,128]{1,0:T(8,128)S(1)}, f32[16,128]{1,0:T(8,128)S(1)}, f32[16,128]{1,0:T(8,128)S(1)}, /*index=5*/f32[16,128]{1,0:T(8,128)S(1)}) fusion(f32[16,128]{1,0:T(8,128)S(1)} %bitcast.553, f32[16,128]{1,0:T(8,128)S(1)} %bitcast.565, f32[16,128]{1,0:T(8,128)S(1)} %bitcast.555, ...), kind=kOutput, calls=%fused_computation.122.clone.1 | convolution fusion | flops 67883008 | bytes 475264 | tf_op jit(solution)/shard_map/while/body/eval_jaxpr/kni,knj->kij/dot_general | solution.py:34
  198.1 5.0 %fusion.202 = (f32[16,128]{1,0:T(8,128)S(1)}, f32[16,128]{1,0:T(8,128)S(1)}, f32[16,128]{1,0:T(8,128)S(1)}, f32[16,128]{1,0:T(8,128)S(1)}, f32[16,128]{1,0:T(8,128)S(1)}, /*index=5*/f32[16,128]{1,0:T(8,128)S(1)}) fusion(f32[16,128]{1,0:T(8,128)S(1)} %bitcast.553, f32[16,128]{1,0:T(8,128)S(1)} %bitcast.565, f32[16,128]{1,0:T(8,128)S(1)} %bitcast.555, ...), kind=kOutput, calls=%fused_computation.122.clone.1 | convolution fusion | flops 67883008 | bytes 475264 | tf_op jit(solution)/shard_map/while/body/eval_jaxpr/kni,knj->kij/dot_general | solution.py:34
  209.1 5.0 %fusion.202 = (f32[16,128]{1,0:T(8,128)S(1)}, f32[16,128]{1,0:T(8,128)S(1)}, f32[16,128]{1,0:T(8,128)S(1)}, f32[16,128]{1,0:T(8,128)S(1)}, f32[16,128]{1,0:T(8,128)S(1)}, /*index=5*/f32[16,128]{1,0:T(8,128)S(1)}) fusion(f32[16,128]{1,0:T(8,128)S(1)} %bitcast.553, f32[16,128]{1,0:T(8,128)S(1)} %bitcast.565, f32[16,128]{1,0:T(8,128)S(1)} %bitcast.555, ...), kind=kOutput, calls=%fused_computation.122.clone.1 | convolution fusion | flops 67883008 | bytes 475264 | tf_op jit(solution)/shard_map/while/body/eval_jaxpr/kni,knj->kij/dot_general | solution.py:34
  221.8 2.3 slice.695
  227.2 5.4 %scatter_fusion.9 = f32[3,2048]{0,1:T(8,128)} fusion(f32[3,2048]{0,1:T(8,128)} %slice.695, s32[512]{0:T(512)S(1)} %bitcast.580, f32[512,3]{1,0:T(8,128)S(1)} %copy.131), kind=kCustom, calls=%fused_computation.44 | custom fusion | flops 1536 | bytes 20480 | tf_op jit(solution)/shard_map/scatter-add | solution.py:134
  233.7 5.3 %scatter_custom_fusion.11 = f32[3,2048]{0,1:T(8,128)} fusion(f32[3,2048]{0,1:T(8,128)} %scatter_fusion.9, s32[512]{0:T(512)} %bitcast.602, f32[3,512]{0,1:T(8,128)S(1)} %collective-permute-done.7), kind=kCustom, calls=%fused_computation.263 | custom fusion | flops 1536 | bytes 30720 | tf_op jit(solution)/shard_map/scatter-add | solution.py:134
  239.1 2.0 multiply_add_fusion.7
  246.1 2.1 collective-permute-start.9
  250.7 76.9 %while.58 = (s32[]{:T(128)}, f32[3,27,128]{2,0,1:T(4,128)S(1)}, s32[7,2,16]{2,1,0:T(2,128)S(1)}, f32[3,27,128]{2,0,1:T(4,128)S(1)}, f32[27,18,128]{2,1,0:T(8,128...) while((s32[]{:T(128)}, f32[3,27,128]{2,0,1:T(4,128)S(1)}, ...), condition=%wide.region_33.34_spmd.clone, body=%wide.region_24.33_spmd.clone.sunk | while | flops 68087472 | bytes 1894617 | solution.py:75
  254.3 5.0 %fusion.211 = (f32[16,128]{1,0:T(8,128)S(1)}, f32[16,128]{1,0:T(8,128)S(1)}, f32[16,128]{1,0:T(8,128)S(1)}, f32[16,128]{1,0:T(8,128)S(1)}, f32[16,128]{1,0:T(8,128)S(1)}, /*index=5*/f32[16,128]{1,0:T(8,128)S(1)}) fusion(f32[16,128]{1,0:T(8,128)S(1)} %bitcast.556, f32[16,128]{1,0:T(8,128)S(1)} %bitcast.568, f32[16,128]{1,0:T(8,128)S(1)} %bitcast.558, ...), kind=kOutput, calls=%fused_computation.168.clone.1 | convolution fusion | flops 67883008 | bytes 475264 | tf_op jit(solution)/shard_map/while/body/eval_jaxpr/kni,knj->kij/dot_general | solution.py:34
  265.3 5.0 %fusion.211 = (f32[16,128]{1,0:T(8,128)S(1)}, f32[16,128]{1,0:T(8,128)S(1)}, f32[16,128]{1,0:T(8,128)S(1)}, f32[16,128]{1,0:T(8,128)S(1)}, f32[16,128]{1,0:T(8,128)S(1)}, /*index=5*/f32[16,128]{1,0:T(8,128)S(1)}) fusion(f32[16,128]{1,0:T(8,128)S(1)} %bitcast.556, f32[16,128]{1,0:T(8,128)S(1)} %bitcast.568, f32[16,128]{1,0:T(8,128)S(1)} %bitcast.558, ...), kind=kOutput, calls=%fused_computation.168.clone.1 | convolution fusion | flops 67883008 | bytes 475264 | tf_op jit(solution)/shard_map/while/body/eval_jaxpr/kni,knj->kij/dot_general | solution.py:34
  276.3 5.0 %fusion.211 = (f32[16,128]{1,0:T(8,128)S(1)}, f32[16,128]{1,0:T(8,128)S(1)}, f32[16,128]{1,0:T(8,128)S(1)}, f32[16,128]{1,0:T(8,128)S(1)}, f32[16,128]{1,0:T(8,128)S(1)}, /*index=5*/f32[16,128]{1,0:T(8,128)S(1)}) fusion(f32[16,128]{1,0:T(8,128)S(1)} %bitcast.556, f32[16,128]{1,0:T(8,128)S(1)} %bitcast.568, f32[16,128]{1,0:T(8,128)S(1)} %bitcast.558, ...), kind=kOutput, calls=%fused_computation.168.clone.1 | convolution fusion | flops 67883008 | bytes 475264 | tf_op jit(solution)/shard_map/while/body/eval_jaxpr/kni,knj->kij/dot_general | solution.py:34
  287.3 5.0 %fusion.211 = (f32[16,128]{1,0:T(8,128)S(1)}, f32[16,128]{1,0:T(8,128)S(1)}, f32[16,128]{1,0:T(8,128)S(1)}, f32[16,128]{1,0:T(8,128)S(1)}, f32[16,128]{1,0:T(8,128)S(1)}, /*index=5*/f32[16,128]{1,0:T(8,128)S(1)}) fusion(f32[16,128]{1,0:T(8,128)S(1)} %bitcast.556, f32[16,128]{1,0:T(8,128)S(1)} %bitcast.568, f32[16,128]{1,0:T(8,128)S(1)} %bitcast.558, ...), kind=kOutput, calls=%fused_computation.168.clone.1 | convolution fusion | flops 67883008 | bytes 475264 | tf_op jit(solution)/shard_map/while/body/eval_jaxpr/kni,knj->kij/dot_general | solution.py:34
  298.3 5.0 %fusion.211 = (f32[16,128]{1,0:T(8,128)S(1)}, f32[16,128]{1,0:T(8,128)S(1)}, f32[16,128]{1,0:T(8,128)S(1)}, f32[16,128]{1,0:T(8,128)S(1)}, f32[16,128]{1,0:T(8,128)S(1)}, /*index=5*/f32[16,128]{1,0:T(8,128)S(1)}) fusion(f32[16,128]{1,0:T(8,128)S(1)} %bitcast.556, f32[16,128]{1,0:T(8,128)S(1)} %bitcast.568, f32[16,128]{1,0:T(8,128)S(1)} %bitcast.558, ...), kind=kOutput, calls=%fused_computation.168.clone.1 | convolution fusion | flops 67883008 | bytes 475264 | tf_op jit(solution)/shard_map/while/body/eval_jaxpr/kni,knj->kij/dot_general | solution.py:34
  309.2 5.0 %fusion.211 = (f32[16,128]{1,0:T(8,128)S(1)}, f32[16,128]{1,0:T(8,128)S(1)}, f32[16,128]{1,0:T(8,128)S(1)}, f32[16,128]{1,0:T(8,128)S(1)}, f32[16,128]{1,0:T(8,128)S(1)}, /*index=5*/f32[16,128]{1,0:T(8,128)S(1)}) fusion(f32[16,128]{1,0:T(8,128)S(1)} %bitcast.556, f32[16,128]{1,0:T(8,128)S(1)} %bitcast.568, f32[16,128]{1,0:T(8,128)S(1)} %bitcast.558, ...), kind=kOutput, calls=%fused_computation.168.clone.1 | convolution fusion | flops 67883008 | bytes 475264 | tf_op jit(solution)/shard_map/while/body/eval_jaxpr/kni,knj->kij/dot_general | solution.py:34
  320.2 5.0 %fusion.211 = (f32[16,128]{1,0:T(8,128)S(1)}, f32[16,128]{1,0:T(8,128)S(1)}, f32[16,128]{1,0:T(8,128)S(1)}, f32[16,128]{1,0:T(8,128)S(1)}, f32[16,128]{1,0:T(8,128)S(1)}, /*index=5*/f32[16,128]{1,0:T(8,128)S(1)}) fusion(f32[16,128]{1,0:T(8,128)S(1)} %bitcast.556, f32[16,128]{1,0:T(8,128)S(1)} %bitcast.568, f32[16,128]{1,0:T(8,128)S(1)} %bitcast.558, ...), kind=kOutput, calls=%fused_computation.168.clone.1 | convolution fusion | flops 67883008 | bytes 475264 | tf_op jit(solution)/shard_map/while/body/eval_jaxpr/kni,knj->kij/dot_general | solution.py:34
  332.2 2.3 slice.710
  335.1 2.0 copy.164
  339.5 2.0 copy.144
  343.3 5.6 %scatter_fusion.10 = f32[3,2048]{0,1:T(8,128)} fusion(f32[3,2048]{0,1:T(8,128)} %slice.710, s32[512]{0:T(512)S(1)} %bitcast.581, f32[512,3]{1,0:T(8,128)} %copy.142), kind=kCustom, calls=%fused_computation.46 | custom fusion | flops 1536 | bytes 20480 | tf_op jit(solution)/shard_map/scatter-add | solution.py:134
  349.2 5.8 %scatter_custom_fusion.13 = f32[3,2048]{0,1:T(8,128)} fusion(f32[3,2048]{0,1:T(8,128)} %scatter_fusion.10, s32[512]{0:T(512)} %bitcast.603, f32[3,512]{0,1:T(8,128)} %collective-permute-done.11), kind=kCustom, calls=%fused_computation.261 | custom fusion | flops 1536 | bytes 286720 | tf_op jit(solution)/shard_map/scatter-add | solution.py:134
  355.1 3.4 multiply_add_fusion.5
  358.5 2.3 gather_fusion.33
  360.9 2.4 collective-permute-start.12
  363.3 2.3 gather_fusion.32
  368.0 3.3 collective-permute-start.13
  373.5 76.9 %while.59 = (s32[]{:T(128)}, f32[3,27,128]{2,0,1:T(4,128)S(1)}, s32[7,2,16]{2,1,0:T(2,128)S(1)}, f32[3,27,128]{2,0,1:T(4,128)S(1)}, f32[27,18,128]{2,1,0:T(8,128...) while((s32[]{:T(128)}, f32[3,27,128]{2,0,1:T(4,128)S(1)}, ...), condition=%wide.region_45.46_spmd.clone, body=%wide.region_36.45_spmd.clone.sunk | while | flops 68087472 | bytes 1894617 | solution.py:75
  377.1 5.0 %fusion.220 = (f32[16,128]{1,0:T(8,128)S(1)}, f32[16,128]{1,0:T(8,128)S(1)}, f32[16,128]{1,0:T(8,128)S(1)}, f32[16,128]{1,0:T(8,128)S(1)}, f32[16,128]{1,0:T(8,128)S(1)}, /*index=5*/f32[16,128]{1,0:T(8,128)S(1)}) fusion(f32[16,128]{1,0:T(8,128)S(1)} %bitcast.559, f32[16,128]{1,0:T(8,128)S(1)} %bitcast.571, f32[16,128]{1,0:T(8,128)S(1)} %bitcast.561, ...), kind=kOutput, calls=%fused_computation.214.clone.1 | convolution fusion | flops 67883008 | bytes 475264 | tf_op jit(solution)/shard_map/while/body/eval_jaxpr/kni,knj->kij/dot_general | solution.py:34
  388.1 5.0 %fusion.220 = (f32[16,128]{1,0:T(8,128)S(1)}, f32[16,128]{1,0:T(8,128)S(1)}, f32[16,128]{1,0:T(8,128)S(1)}, f32[16,128]{1,0:T(8,128)S(1)}, f32[16,128]{1,0:T(8,128)S(1)}, /*index=5*/f32[16,128]{1,0:T(8,128)S(1)}) fusion(f32[16,128]{1,0:T(8,128)S(1)} %bitcast.559, f32[16,128]{1,0:T(8,128)S(1)} %bitcast.571, f32[16,128]{1,0:T(8,128)S(1)} %bitcast.561, ...), kind=kOutput, calls=%fused_computation.214.clone.1 | convolution fusion | flops 67883008 | bytes 475264 | tf_op jit(solution)/shard_map/while/body/eval_jaxpr/kni,knj->kij/dot_general | solution.py:34
  399.1 5.0 %fusion.220 = (f32[16,128]{1,0:T(8,128)S(1)}, f32[16,128]{1,0:T(8,128)S(1)}, f32[16,128]{1,0:T(8,128)S(1)}, f32[16,128]{1,0:T(8,128)S(1)}, f32[16,128]{1,0:T(8,128)S(1)}, /*index=5*/f32[16,128]{1,0:T(8,128)S(1)}) fusion(f32[16,128]{1,0:T(8,128)S(1)} %bitcast.559, f32[16,128]{1,0:T(8,128)S(1)} %bitcast.571, f32[16,128]{1,0:T(8,128)S(1)} %bitcast.561, ...), kind=kOutput, calls=%fused_computation.214.clone.1 | convolution fusion | flops 67883008 | bytes 475264 | tf_op jit(solution)/shard_map/while/body/eval_jaxpr/kni,knj->kij/dot_general | solution.py:34
  410.1 5.0 %fusion.220 = (f32[16,128]{1,0:T(8,128)S(1)}, f32[16,128]{1,0:T(8,128)S(1)}, f32[16,128]{1,0:T(8,128)S(1)}, f32[16,128]{1,0:T(8,128)S(1)}, f32[16,128]{1,0:T(8,128)S(1)}, /*index=5*/f32[16,128]{1,0:T(8,128)S(1)}) fusion(f32[16,128]{1,0:T(8,128)S(1)} %bitcast.559, f32[16,128]{1,0:T(8,128)S(1)} %bitcast.571, f32[16,128]{1,0:T(8,128)S(1)} %bitcast.561, ...), kind=kOutput, calls=%fused_computation.214.clone.1 | convolution fusion | flops 67883008 | bytes 475264 | tf_op jit(solution)/shard_map/while/body/eval_jaxpr/kni,knj->kij/dot_general | solution.py:34
  421.1 5.0 %fusion.220 = (f32[16,128]{1,0:T(8,128)S(1)}, f32[16,128]{1,0:T(8,128)S(1)}, f32[16,128]{1,0:T(8,128)S(1)}, f32[16,128]{1,0:T(8,128)S(1)}, f32[16,128]{1,0:T(8,128)S(1)}, /*index=5*/f32[16,128]{1,0:T(8,128)S(1)}) fusion(f32[16,128]{1,0:T(8,128)S(1)} %bitcast.559, f32[16,128]{1,0:T(8,128)S(1)} %bitcast.571, f32[16,128]{1,0:T(8,128)S(1)} %bitcast.561, ...), kind=kOutput, calls=%fused_computation.214.clone.1 | convolution fusion | flops 67883008 | bytes 475264 | tf_op jit(solution)/shard_map/while/body/eval_jaxpr/kni,knj->kij/dot_general | solution.py:34
  432.0 5.0 %fusion.220 = (f32[16,128]{1,0:T(8,128)S(1)}, f32[16,128]{1,0:T(8,128)S(1)}, f32[16,128]{1,0:T(8,128)S(1)}, f32[16,128]{1,0:T(8,128)S(1)}, f32[16,128]{1,0:T(8,128)S(1)}, /*index=5*/f32[16,128]{1,0:T(8,128)S(1)}) fusion(f32[16,128]{1,0:T(8,128)S(1)} %bitcast.559, f32[16,128]{1,0:T(8,128)S(1)} %bitcast.571, f32[16,128]{1,0:T(8,128)S(1)} %bitcast.561, ...), kind=kOutput, calls=%fused_computation.214.clone.1 | convolution fusion | flops 67883008 | bytes 475264 | tf_op jit(solution)/shard_map/while/body/eval_jaxpr/kni,knj->kij/dot_general | solution.py:34
  443.0 5.0 %fusion.220 = (f32[16,128]{1,0:T(8,128)S(1)}, f32[16,128]{1,0:T(8,128)S(1)}, f32[16,128]{1,0:T(8,128)S(1)}, f32[16,128]{1,0:T(8,128)S(1)}, f32[16,128]{1,0:T(8,128)S(1)}, /*index=5*/f32[16,128]{1,0:T(8,128)S(1)}) fusion(f32[16,128]{1,0:T(8,128)S(1)} %bitcast.559, f32[16,128]{1,0:T(8,128)S(1)} %bitcast.571, f32[16,128]{1,0:T(8,128)S(1)} %bitcast.561, ...), kind=kOutput, calls=%fused_computation.214.clone.1 | convolution fusion | flops 67883008 | bytes 475264 | tf_op jit(solution)/shard_map/while/body/eval_jaxpr/kni,knj->kij/dot_general | solution.py:34
  454.3 2.7 collective-permute-done.14
  458.0 5.2 %scatter_fusion.11 = f32[3,2048]{0,1:T(8,128)} fusion(f32[3,2048]{0,1:T(8,128)} %slice.725, s32[512]{0:T(512)S(1)} %bitcast.582, f32[512,3]{1,0:T(8,128)S(1)} %copy.153), kind=kCustom, calls=%fused_computation.48 | custom fusion | flops 1536 | bytes 20480 | tf_op jit(solution)/shard_map/scatter-add | solution.py:134
  464.6 5.4 %scatter_custom_fusion.15 = f32[3,2048]{0,1:T(8,128)} fusion(f32[3,2048]{0,1:T(8,128)} %scatter_fusion.11, s32[512]{0:T(512)} %bitcast.604, f32[3,512]{0,1:T(8,128)S(1)} %collective-permute-done.15), kind=kCustom, calls=%fused_computation.259 | custom fusion | flops 1536 | bytes 30720 | tf_op jit(solution)/shard_map/scatter-add | solution.py:134
  470.0 2.5 fusion.92
  472.5 2.2 copy.156
  (813 shorter events, 227.7 us)
Async XLA Ops:
  0.6 20.8 %copy-start = (f32[18]{0:T(128)S(1)}, f32[18]{0:T(128)}, u32[]{:S(2)}) copy-start(f32[18]{0:T(128)} %param.36) | copy-start | bytes 220
  0.6 4.8 %copy-start.21 = (f32[3,1,1,2048]{3,2,1,0:T(1,128)S(1)}, f32[3,1,1,2048]{3,2,1,0:T(1,128)}, u32[]{:S(2)}) copy-start(f32[3,1,1,2048]{3,2,1,0:T(1,128)} %param.32) | copy-start | bytes 73732
  2.0 5.0 %copy-start.23 = (s32[512,1]{0,1:T(1,128)}, s32[512,1]{0,1:T(1,128)S(1)}, u32[]{:S(2)}) copy-start(s32[512,1]{0,1:T(1,128)S(1)} %compare_select_fusion.8) | copy-start | bytes 6148
  2.0 5.0 %copy-start.9 = (s32[1024]{0:T(1024)}, s32[1024]{0:T(1024)S(1)}, u32[]{:S(2)}) copy-start(s32[1024]{0:T(1024)S(1)} %get-tuple-element.754) | copy-start | bytes 12292
  2.1 12.0 %copy-start.6 = (s32[1024]{0:T(1024)}, s32[1024]{0:T(1024)S(1)}, u32[]{:S(2)}) copy-start(s32[1024]{0:T(1024)S(1)} %get-tuple-element.755) | copy-start | bytes 12292
  5.5 5.4 %copy-start.12 = (f32[18,18]{1,0:T(8,128)S(1)}, f32[18,18]{1,0:T(8,128)}, u32[]{:S(2)}) copy-start(f32[18,18]{1,0:T(8,128)} %param.35) | copy-start | bytes 3892
  5.5 5.5 %copy-start.1 = (s32[1,1,2048]{2,1,0:T(1,128)S(1)}, s32[1,1,2048]{2,1,0:T(1,128)}, u32[]{:S(2)}) copy-start(s32[1,1,2048]{2,1,0:T(1,128)} %param.34) | copy-start | bytes 24580
  7.1 8.5 %copy-start.13 = (f32[3]{0:T(128)S(1)}, f32[3]{0:T(128)}, u32[]{:S(2)}) copy-start(f32[3]{0:T(128)} %constant.389.clone) | copy-start | bytes 40
  7.1 8.2 %collective-permute-start = (f32[4,512]{1,0:T(4,128)S(1)}, f32[4,512]{1,0:T(4,128)S(1)}, u32[]{:S(2)}, u32[]{:S(2)}) collective-permute-start(f32[4,512]{1,0:T(4,128)S(1)} %pad_maximum_fusion.7), channel_id=1, source_target_pairs={{0,7},{1,0},{2,1},{3,2},{4,3},{5,4},{6,5},{7,6},{8,15},{9,8},{10,9... | collective-permute-start | bytes 24584 | tf_op jit(solution)/shard_map/ppermute | solution.py:22
  10.8 8.9 %copy-start.24 = (s32[1,1,2,112]{3,2,1,0:T(2,128)S(1)}, s32[1,1,2,112]{3,2,1,0:T(2,128)}, u32[]{:S(2)}) copy-start(s32[1,1,2,112]{3,2,1,0:T(2,128)} %param.39) | copy-start | bytes 2692
  10.8 10.9 %copy-start.17 = (f32[3]{0:T(128)S(1)}, f32[3]{0:T(128)}, u32[]{:S(2)}) copy-start(f32[3]{0:T(128)} %constant.388.clone) | copy-start | bytes 40
  10.9 11.0 %copy-start.5 = (f32[3,256]{1,0:T(4,128)S(1)}, f32[3,256]{1,0:T(4,128)}, u32[]{:S(2)}) copy-start(f32[3,256]{1,0:T(4,128)} %constant.383.clone.1) | copy-start | bytes 9220
  16.0 5.0 %collective-permute-start.1 = (f32[4,640]{1,0:T(4,128)S(1)}, f32[4,640]{1,0:T(4,128)S(1)}, u32[]{:S(2)}, u32[]{:S(2)}) collective-permute-start(f32[4,640]{1,0:T(4,128)S(1)} %fusion.118), channel_id=1, source_target_pairs={{0,24},{8,0},{16,8},{24,16},{1,25},{9,1},{17,9},{25,17},{2,26},{10... | collective-permute-start | bytes 30728 | tf_op jit(solution)/shard_map/ppermute | solution.py:22
  98.9 4.2 copy-start.22
  102.8 5.8 %collective-permute-start.2 = (f32[3,640]{1,0:T(4,128)S(1)}, f32[3,640]{1,0:T(4,128)S(1)}, u32[]{:S(2)}, u32[]{:S(2)}) collective-permute-start(f32[3,640]{1,0:T(4,128)S(1)} %pad_maximum_fusion.8), channel_id=1, source_target_pairs={{0,8},{8,16},{16,24},{24,0},{1,9},{9,17},{17,25},{25,1},{2,10},{10... | collective-permute-start | bytes 23048 | tf_op jit(solution)/shard_map/ppermute | solution.py:22
  103.5 21.5 %copy-start.2 = (f32[3,1,1,2048]{0,3,2,1:T(8,128)}, f32[3,1,1,2048]{0,3,2,1:T(8,128)S(1)}, u32[]{:S(2)}) copy-start(f32[3,1,1,2048]{0,3,2,1:T(8,128)S(1)} %copy.110) | copy-start | bytes 73732
  113.9 6.9 %collective-permute-start.3 = (f32[3,512]{0,1:T(8,128)S(1)}, f32[3,512]{0,1:T(8,128)}, u32[]{:S(2)}, u32[]{:S(2)}) collective-permute-start(f32[3,512]{0,1:T(8,128)S(1)} %bitcast.504), channel_id=1, source_target_pairs={{0,1},{1,2},{2,3},{3,4},{4,5},{5,6},{6,7},{7,0},{8,9},{9,10},{10,1... | collective-permute-start | bytes 18440 | tf_op jit(solution)/shard_map/ppermute | solution.py:22
  125.0 1.2 copy-start.10
  125.0 4.5 copy-start.7
  126.3 7.2 %copy-start.14 = (f32[3]{0:T(128)S(1)}, f32[3]{0:T(128)}, u32[]{:S(2)}) copy-start(f32[3]{0:T(128)} %constant.389.clone) | copy-start | bytes 40
  126.3 13.1 %copy-start.18 = (f32[3]{0:T(128)S(1)}, f32[3]{0:T(128)}, u32[]{:S(2)}) copy-start(f32[3]{0:T(128)} %constant.388.clone) | copy-start | bytes 40
  128.7 4.8 %collective-permute-start.4 = (f32[4,512]{1,0:T(4,128)S(1)}, f32[4,512]{1,0:T(4,128)S(1)}, u32[]{:S(2)}, u32[]{:S(2)}) collective-permute-start(f32[4,512]{1,0:T(4,128)S(1)} %pad_maximum_fusion.6), channel_id=1, source_target_pairs={{0,7},{1,0},{2,1},{3,2},{4,3},{5,4},{6,5},{7,6},{8,15},{9,8},{10,9... | collective-permute-start | bytes 24584 | tf_op jit(solution)/shard_map/ppermute | solution.py:22
  134.2 4.5 collective-permute-start.5
  220.4 5.8 %collective-permute-start.6 = (f32[3,640]{1,0:T(4,128)S(1)}, f32[3,640]{1,0:T(4,128)S(1)}, u32[]{:S(2)}, u32[]{:S(2)}) collective-permute-start(f32[3,640]{1,0:T(4,128)S(1)} %pad_maximum_fusion.9), channel_id=1, source_target_pairs={{0,8},{8,16},{16,24},{24,0},{1,9},{9,17},{17,25},{25,1},{2,10},{10... | collective-permute-start | bytes 23048 | tf_op jit(solution)/shard_map/ppermute | solution.py:22
  227.0 6.7 %collective-permute-start.7 = (f32[3,512]{0,1:T(8,128)S(1)}, f32[3,512]{0,1:T(8,128)S(1)}, u32[]{:S(2)}, u32[]{:S(2)}) collective-permute-start(f32[3,512]{0,1:T(8,128)S(1)} %bitcast.507), channel_id=1, source_target_pairs={{0,1},{1,2},{2,3},{3,4},{4,5},{5,6},{6,7},{7,0},{8,9},{9,10},{10,1... | collective-permute-start | bytes 18440 | tf_op jit(solution)/shard_map/ppermute | solution.py:22
  239.1 2.0 copy-start.11
  239.1 4.8 copy-start.8
  241.1 4.3 copy-start.15
  241.1 9.3 %copy-start.19 = (f32[3]{0:T(128)S(1)}, f32[3]{0:T(128)}, u32[]{:S(2)}) copy-start(f32[3]{0:T(128)} %constant.388.clone) | copy-start | bytes 40
  242.3 3.1 collective-permute-start.8
  246.1 3.7 collective-permute-start.9
  331.5 5.6 %collective-permute-start.10 = (f32[3,640]{1,0:T(4,128)S(1)}, f32[3,640]{1,0:T(4,128)S(1)}, u32[]{:S(2)}, u32[]{:S(2)}) collective-permute-start(f32[3,640]{1,0:T(4,128)S(1)} %pad_maximum_fusion.10), channel_id=1, source_target_pairs={{0,8},{8,16},{16,24},{24,0},{1,9},{9,17},{17,25},{25,1},{2,10},{10... | collective-permute-start | bytes 23048 | tf_op jit(solution)/shard_map/ppermute | solution.py:22
  334.5 20.6 %copy-start.3 = (f32[3,1,1,2048]{0,3,2,1:T(8,128)S(1)}, f32[3,1,1,2048]{0,3,2,1:T(8,128)}, u32[]{:S(2)}) copy-start(f32[3,1,1,2048]{0,3,2,1:T(8,128)} %copy-done.2) | copy-start | bytes 73732
  342.4 6.9 %collective-permute-start.11 = (f32[3,512]{0,1:T(8,128)S(1)}, f32[3,512]{0,1:T(8,128)}, u32[]{:S(2)}, u32[]{:S(2)}) collective-permute-start(f32[3,512]{0,1:T(8,128)S(1)} %bitcast.510), channel_id=1, source_target_pairs={{0,1},{1,2},{2,3},{3,4},{4,5},{5,6},{6,7},{7,0},{8,9},{9,10},{10,1... | collective-permute-start | bytes 18440 | tf_op jit(solution)/shard_map/ppermute | solution.py:22
  358.5 8.7 %copy-start.16 = (f32[3]{0:T(128)S(1)}, f32[3]{0:T(128)}, u32[]{:S(2)}) copy-start(f32[3]{0:T(128)} %constant.389.clone) | copy-start | bytes 40
  358.5 14.7 %copy-start.20 = (f32[3]{0:T(128)S(1)}, f32[3]{0:T(128)}, u32[]{:S(2)}) copy-start(f32[3]{0:T(128)} %constant.388.clone) | copy-start | bytes 40
  360.9 6.3 %collective-permute-start.12 = (f32[4,512]{1,0:T(4,128)S(1)}, f32[4,512]{1,0:T(4,128)S(1)}, u32[]{:S(2)}, u32[]{:S(2)}) collective-permute-start(f32[4,512]{1,0:T(4,128)S(1)} %pad_maximum_fusion.4), channel_id=1, source_target_pairs={{0,7},{1,0},{2,1},{3,2},{4,3},{5,4},{6,5},{7,6},{8,15},{9,8},{10,9... | collective-permute-start | bytes 24584 | tf_op jit(solution)/shard_map/ppermute | solution.py:22
  368.0 4.6 collective-permute-start.13
  451.2 5.8 %collective-permute-start.14 = (f32[3,640]{1,0:T(4,128)S(1)}, f32[3,640]{1,0:T(4,128)S(1)}, u32[]{:S(2)}, u32[]{:S(2)}) collective-permute-start(f32[3,640]{1,0:T(4,128)S(1)} %pad_maximum_fusion.11), channel_id=1, source_target_pairs={{0,8},{8,16},{16,24},{24,0},{1,9},{9,17},{17,25},{25,1},{2,10},{10... | collective-permute-start | bytes 23048 | tf_op jit(solution)/shard_map/ppermute | solution.py:22
  453.8 16.2 %copy-start.4 = (f32[3,2048]{0,1:T(8,128)S(1)}, f32[3,2048]{0,1:T(8,128)}, u32[]{:S(2)}) copy-start(f32[3,2048]{0,1:T(8,128)} %get-tuple-element.695) | copy-start | bytes 73732
  457.8 6.7 %collective-permute-start.15 = (f32[3,512]{0,1:T(8,128)S(1)}, f32[3,512]{0,1:T(8,128)S(1)}, u32[]{:S(2)}, u32[]{:S(2)}) collective-permute-start(f32[3,512]{0,1:T(8,128)S(1)} %bitcast.513), channel_id=1, source_target_pairs={{0,1},{1,2},{2,3},{3,4},{4,5},{5,6},{6,7},{7,0},{8,9},{9,10},{10,1... | collective-permute-start | bytes 18440 | tf_op jit(solution)/shard_map/ppermute | solution.py:22
where the time goes:
time: 485 us; the launch traced here: 476 us
  local copies, waits for them, and re-layouts  165 us (34%)
  matrix products  143 us (29%)
  other arithmetic  122 us (25%)
  starting transfers between devices  24.4 us (5%)
  waiting for transfers between devices  15.3 us (3%)
    dot_general x28, matrix products, pair_block(): jnp.einsum('kni,knj->kij', eps_rows, onehot_b, precision=lax.Precision.HI...  141 us
    scatter-add x8, other arithmetic, step_forces(): return f_home.at[:, x_index].add(own_x).at[:, y_index].add(own_y)  41.1 us
    scatter-add x28, other arithmetic, one_block(): summed = summed.at[:, right_ids].add(on_b)  31.4 us
    scatter-add x28, other arithmetic, one_block(): summed = summed.at[:, left_ids].add(on_a)  31 us
    ppermute x16, starting transfers between devices, from_behind(): lax.ppermute(array, axis, [(i, (i + by) % peers) for i in range(peers)])  24.4 us
    gather x28, local copies, waits for them, and re-layouts, one_block(): pos_zone[:, right_ids]  16.5 us
    gather x28, local copies, waits for them, and re-layouts, one_block(): pos_zone[:, left_ids]  16.5 us
    gather x28, local copies, waits for them, and re-layouts, one_block(): onehot[right_ids]  15.8 us
  transfers between devices with their start and end apart: 16, of which 11 were waited for; matrix products, arithmetic and copies ran while one was open for 11% of the time, Pallas kernels for 0%

commit v1 on v0

v1 whole, which is shorter than its diff:
```python
import functools

import jax
import jax.numpy as jnp
from jax import lax
from jax.experimental import pallas as pl
from jax.experimental.pallas import tpu as pltpu
from jax.sharding import PartitionSpec as P

NTYPES = 18
STEPS = 4
SPACING = 0.43
CUTOFF = 1.1
SIGMA = 0.41
COULOMB = 138.935458 / 15.0
MASS = 72.0
TIME_STEP = 0.02

MESH = pl.DeviceIdType.MESH
ROWS = 16
LANES = 128
HALO = 8
NONE = 31
SIDES = [(-1, -1), (-1, 0), (-1, 1), (0, -1), (0, 1), (1, -1), (1, 0), (1, 1)]
ZONES = [(0, 0), (1, 0), (0, 1), (1, 1)]
SHIFTS = [(dx, dy) for dy in range(-2, 3) for dx in range(-2, 3)]
OFFSETS = [
    (number, dz)
    for number, (dx, dy) in enumerate(SHIFTS)
    for dz in range(-2, 3)
    if 0 < dx * dx + dy * dy + dz * dz <= 8
]


def lane_gather(values, index):
    return jnp.take_along_axis(values, index, axis=1)


def kernel(
    n_gx, n_gy, side,
    pos_ref, vel_ref, kind_ref, tile_ref, table_ref,
    out_pos_ref, out_vel_ref,
    tile_send, tile_recv, send, recv, ext, kind_ext, coef_lj, coef_q, now, speed, mix, site_ref,
    tile_sems, send_sems, recv_sems,
):
    width = side * SPACING
    my_x = lax.axis_index("gx")
    my_y = lax.axis_index("gy")

    def at(sx, sy):
        return (
            lax.rem(my_x + (sx + n_gx), n_gx),
            lax.rem(my_y + (sy + n_gy), n_gy),
        )

    barrier = pltpu.get_barrier_semaphore()
    for sx, sy in SIDES:
        pl.semaphore_signal(barrier, inc=1, device_id=at(sx, sy), device_id_type=MESH)

    lane = lax.broadcasted_iota(jnp.int32, (ROWS, LANES), 1)
    row = lax.broadcasted_iota(jnp.int32, (ROWS, LANES), 0)
    lane8 = lane[:8]
    half = lane >> 6
    y_site = (lane >> 3) & 7
    x_site = lane & 7
    low_half = lane8 < 64

    tile_send[...] = jnp.full((8, LANES), NONE - 1, jnp.int32)
    tile_send[0:2, 0 : tile_ref.shape[1]] = tile_ref[...]

    cluster = row
    sx_f = jnp.floor(pos_ref[0] * (1.0 / SPACING) + 0.5)
    sy_f = jnp.floor(pos_ref[1] * (1.0 / SPACING) + 0.5)
    sz_f = jnp.floor(pos_ref[2] * (1.0 / SPACING) + 0.5)
    site = (
        (sz_f.astype(jnp.int32) - 2 * cluster) * 64
        + sy_f.astype(jnp.int32) * 8
        + sx_f.astype(jnp.int32)
    )
    site = jnp.clip(site, 0, LANES - 1)
    site_ref[...] = site
    big_row = lax.broadcasted_iota(jnp.int32, (LANES, LANES), 0)
    row8 = row[:8]
    parts = []
    for part in range(2):
        total = jnp.zeros((8, LANES), jnp.float32)
        for sub in range(8):
            here = site[part * 8 + sub : part * 8 + sub + 1, :]
            onehot = jnp.where(big_row == here, 1.0, 0.0).astype(jnp.bfloat16)
            left = jnp.where(row8 == sub, lane8, 0).astype(jnp.float32).astype(jnp.bfloat16)
            total = total + lax.dot_general(
                left, onehot, (((1,), (1,)), ((), ())), preferred_element_type=jnp.float32
            )
        parts.append(total)
    slot = jnp.concatenate(parts, axis=0).astype(jnp.int32)

    def to_lattice(values):
        ordered = lane_gather(values, slot)
        first, second = ordered[:8], ordered[8:]
        even = jnp.where(low_half, first, pltpu.roll(second, 64, 1))
        odd = jnp.where(low_half, pltpu.roll(first, 64, 1), second)
        mix[pl.ds(0, 8, stride=2), :] = even
        mix[pl.ds(1, 8, stride=2), :] = odd
        return mix[...]

    def to_slots(values):
        mix[...] = values
        even = mix[pl.ds(0, 8, stride=2), :]
        odd = mix[pl.ds(1, 8, stride=2), :]
        first = jnp.where(low_half, even, pltpu.roll(odd, 64, 1))
        second = jnp.where(low_half, pltpu.roll(even, 64, 1), odd)
        return lane_gather(jnp.concatenate([first, second], axis=0), site_ref[...])

    for component in range(3):
        now[component] = to_lattice(pos_ref[component])
        speed[component] = to_lattice(vel_ref[component])
    kind = to_lattice(kind_ref[...].astype(jnp.float32))

    def pack_index(sx, sy):
        if sx != 0 and sy != 0:
            slot_of = lane >> 3
            inner = lane & 7
            zh, yb, xb = inner >> 2, (inner >> 1) & 1, inner & 1
        elif sx != 0:
            slot_of = lane >> 5
            inner = lane & 31
            zh, yb, xb = inner >> 4, (inner >> 1) & 7, inner & 1
        else:
            slot_of = lane >> 5
            inner = lane & 31
            zh, yb, xb = inner >> 4, (inner >> 3) & 1, inner & 7
        x_low = side - 2 if sx > 0 else 0
        y_low = side - 2 if sy > 0 else 0
        return slot_of, zh * 64 + (yb + y_low) * 8 + xb + x_low

    def unpack_index(sx, sy):
        if sx != 0 and sy != 0:
            return half * 4 + (y_site & 1) * 2 + (x_site & 1), 8
        if sx != 0:
            return half * 16 + y_site * 2 + (x_site & 1), 32
        return half * 16 + (y_site & 1) * 8 + x_site, 32

    def pack(values, sx, sy):
        slot_of, source = pack_index(sx, sy)
        packed = lane_gather(values[0], source)
        for component in range(1, len(values)):
            packed = jnp.where(slot_of == component, lane_gather(values[component], source), packed)
        return packed

    def side_copy(turn, number):
        sx, sy = SIDES[number]
        return pltpu.make_async_remote_copy(
            src_ref=send.at[turn, number],
            dst_ref=recv.at[turn, number],
            send_sem=send_sems.at[turn, number],
            recv_sem=recv_sems.at[turn, number],
            device_id=at(sx, sy),
            device_id_type=MESH,
        )

    def tile_copy(number):
        sx, sy = ZONES[number + 1]
        return pltpu.make_async_remote_copy(
            src_ref=tile_send,
            dst_ref=tile_recv.at[number],
            send_sem=tile_sems.at[0, number],
            recv_sem=tile_sems.at[1, number],
            device_id=at(sx, sy),
            device_id_type=MESH,
        )

    def image(turn, ux, uy, component):
        number = SIDES.index((-ux, -uy))
        index, stride = unpack_index(ux, uy)
        return lane_gather(recv[turn, number], index + component * stride)

    def merge_and_shift(images, dx, dy):
        merged = images[(0, 0)]
        in_x = (x_site < dx) if dx > 0 else (x_site >= side + dx)
        in_y = (y_site < dy) if dy > 0 else (y_site >= side + dy)
        ux = (dx > 0) - (dx < 0)
        uy = (dy > 0) - (dy < 0)
        if dx != 0:
            merged = jnp.where(in_x, images[(ux, 0)], merged)
        if dy != 0:
            outer = images[(0, uy)]
            if dx != 0:
                outer = jnp.where(in_x, images[(ux, uy)], outer)
            merged = jnp.where(in_y, outer, merged)
        if dx == 0 and dy == 0:
            return merged
        source = half * 64 + ((y_site + dy) & 7) * 8 + ((x_site + dx) & 7)
        return lane_gather(merged, source)

    def put_extended(ref, values):
        ref[pl.ds(HALO, ROWS), :] = values
        ref[pl.ds(0, HALO), :] = pltpu.roll(values[8:], 64, 1)
        ref[pl.ds(HALO + ROWS, HALO), :] = pltpu.roll(values[:8], 64, 1)

    def gather_images(turn, component, own):
        shift_of = (width, width, 0.0, 0.0)
        images = {(0, 0): own}
        for ux, uy in SIDES:
            got = image(turn, ux, uy, component)
            if component == 0 and ux != 0:
                got = got + ux * width
            if component == 1 and uy != 0:
                got = got + uy * width
            images[(ux, uy)] = got
        return images

    def exchange(turn, values):
        for number, (sx, sy) in enumerate(SIDES):
            send[turn, number] = pack(values, sx, sy)
        for number in range(len(SIDES)):
            side_copy(turn, number).start()

    def spread_positions(turn, own):
        for component in range(3):
            images = gather_images(turn, component, own[component])
            for number, (dx, dy) in enumerate(SHIFTS):
                put_extended(ext.at[number, component], merge_and_shift(images, dx, dy))

    pl.semaphore_wait(barrier, len(SIDES))
    own = [now[component] for component in range(3)]
    exchange(0, own + [kind])
    for number in range(3):
        tile_copy(number).start()
    for number in range(len(SIDES)):
        side_copy(0, number).wait_recv()
    for number in range(3):
        tile_copy(number).wait_recv()

    iota_small = lax.broadcasted_iota(jnp.int32, (32, LANES), 0)
    lane_small = lax.broadcasted_iota(jnp.int32, (32, LANES), 1)
    count_row = lax.broadcasted_iota(jnp.int32, (ROWS, 32), 0)
    count_lane = lax.broadcasted_iota(jnp.int32, (ROWS, 32), 1)
    nt = (((1,), (1,)), ((), ()))

    def onehot_of(condition):
        return jnp.where(condition, 1.0, 0.0).astype(jnp.bfloat16)

    tables = []
    for pair in range(2):
        table = jnp.zeros((ROWS, LANES), jnp.float32)
        for zone in (2 * pair, 2 * pair + 1):
            source = tile_send if zone == 0 else tile_recv.at[zone - 1]
            first = source[0:1, :]
            second = source[1:2, :]
            base = 32 * (zone & 1)
            small_a = onehot_of(iota_small == first)
            small_b = onehot_of(iota_small == second)
            place = big_row - base
            big_a = onehot_of((place == first) | (place == first + 64))
            big_b = onehot_of((place == second) | (place == second + 64))
            forth = lax.dot_general(small_a, big_b, nt, preferred_element_type=jnp.float32)
            back = lax.dot_general(small_b, big_a, nt, preferred_element_type=jnp.float32)
            on_diagonal = (lane_small & 63) == iota_small + base
            counts = jnp.where(on_diagonal, forth, forth + back).astype(jnp.bfloat16)
            picked = []
            for zh in range(2):
                layer = zh * ROWS + count_row
                if zone == 0:
                    which = layer >> 1
                elif zone == 1:
                    which = 16 + (layer >> 3)
                elif zone == 2:
                    which = 20 + (layer >> 3)
                else:
                    which = jnp.full_like(layer, 24)
                picked.append(
                    jnp.dot(onehot_of(count_lane == which), counts, preferred_element_type=jnp.float32)
                )
            table = table + jnp.where(half == 0, picked[0], picked[1])
        tables.append(table)

    kind_images = gather_images(0, 3, kind)
    kind_own = kind.astype(jnp.int32)
    eps_rows = [jnp.broadcast_to(table_ref[k : k + 1, :], (ROWS, LANES)) for k in range(4)]
    charge_own = lane_gather(eps_rows[3], kind_own)
    for number, (dx, dy) in enumerate(SHIFTS):
        put_extended(kind_ext.at[number], merge_and_shift(kind_images, dx, dy))

    zone_of = []
    for number, (dx, dy) in enumerate(SHIFTS):
        masks = []
        for ox, oy in ZONES:
            px, py = x_site + ox * side, y_site + oy * side
            qx, qy = px + dx, py + dy
            limit = side + 2
            inside = (px < limit) & (py < limit) & (qx >= 0) & (qx < limit) & (qy >= 0) & (qy < limit)
            in_x, in_y = qx >= side, qy >= side
            start = jnp.where(in_x, jnp.where(in_y, 24, 16), jnp.where(in_y, 20, 0))
            shift = jnp.where(in_x, jnp.where(in_y, 6, 3), jnp.where(in_y, 3, 1))
            masks.append((inside, start, shift))
        for dz in range(-2, 3):
            if (number, dz) not in OFFSETS:
                continue
            place = OFFSETS.index((number, dz))
            layer = half * ROWS + row + dz
            in_z = (layer >= 0) & (layer < 2 * ROWS)
            weight = jnp.zeros((ROWS, LANES), jnp.float32)
            for zone in range(4):
                ox, oy = ZONES[zone]
                inside, start, shift = masks[zone]
                which = jnp.where(inside & in_z, start + (layer >> shift), NONE)
                weight = weight + lane_gather(
                    tables[zone >> 1], half * 64 + 32 * (zone & 1) + which
                )
            other = kind_ext[number, pl.ds(HALO + dz, ROWS), :].astype(jnp.int32)
            pair = kind_own * (NTYPES + 1) + other
            low = pair & (LANES - 1)
            high = pair >> 7
            depth = jnp.where(
                high == 0,
                lane_gather(eps_rows[0], low),
                jnp.where(high == 1, lane_gather(eps_rows[1], low), lane_gather(eps_rows[2], low)),
            )
            coef_lj[place] = weight * depth * (24.0 * SIGMA**6)
            coef_q[place] = weight * (COULOMB * charge_own) * lane_gather(eps_rows[3], other)

    def advance(turn):
        mine = [now[component] for component in range(3)]
        spread_positions(turn, mine)
        force = [jnp.zeros((ROWS, LANES), jnp.float32) for _ in range(3)]
        for place, (number, dz) in enumerate(OFFSETS):
            apart = [mine[k] - ext[number, k, pl.ds(HALO + dz, ROWS), :] for k in range(3)]
            dist_sq = apart[0] * apart[0] + apart[1] * apart[1] + apart[2] * apart[2]
            inv_r = lax.rsqrt(dist_sq)
            inv_sq = inv_r * inv_r
            switch = jnp.maximum(1.0 - dist_sq * (1.0 / (CUTOFF * CUTOFF)), 0.0)
            inv_4 = inv_sq * inv_sq
            inv_6 = inv_4 * inv_sq
            lennard = coef_lj[place] * (inv_4 * inv_4) * (inv_6 * (2.0 * SIGMA**6) - 1.0)
            coulomb = coef_q[place] * (inv_sq * inv_r - 1.0 / CUTOFF**3)
            scalar = switch * switch * (lennard + coulomb)
            for k in range(3):
                force[k] = force[k] + scalar * apart[k]
        for k in range(3):
            new_speed = speed[k] + (TIME_STEP / MASS) * force[k]
            speed[k] = new_speed
            now[k] = mine[k] + TIME_STEP * new_speed

    def turn_body(turn, carry):
        advance(turn)
        exchange(turn + 1, [now[component] for component in range(3)])
        for number in range(len(SIDES)):
            side_copy(turn + 1, number).wait_recv()
        return carry

    lax.fori_loop(0, STEPS - 1, turn_body, 0)
    advance(STEPS - 1)
    for component in range(3):
        out_pos_ref[component] = to_slots(now[component])
        out_vel_ref[component] = to_slots(speed[component])
    for turn in range(STEPS):
        for number in range(len(SIDES)):
            side_copy(turn, number).wait_send()
    for number in range(3):
        tile_copy(number).wait_send()


def per_device(n_gx, n_gy, positions, velocities, bead_types, eps_table, charges, x_list, y_list, tiles):
    beads = positions.shape[-1]
    strip = x_list.shape[-1]
    side = 2 * beads // strip
    eps_sym = 0.5 * (eps_table + eps_table.T)
    flat = jnp.pad(eps_sym, ((0, 1), (0, 1))).reshape(-1)
    flat = jnp.pad(flat, (0, 3 * LANES - flat.shape[0])).reshape(3, LANES)
    charge_row = jnp.pad(charges, (0, LANES - charges.shape[0]))[None]
    table = jnp.concatenate([flat, charge_row, jnp.zeros((4, LANES), jnp.float32)], axis=0)
    shape = jax.ShapeDtypeStruct((3, ROWS, LANES), jnp.float32)
    vmem = pl.BlockSpec(memory_space=pltpu.VMEM)
    new_pos, new_vel = pl.pallas_call(
        functools.partial(kernel, n_gx, n_gy, side),
        out_shape=(shape, shape),
        in_specs=[vmem] * 5,
        out_specs=(vmem, vmem),
        scratch_shapes=[
            pltpu.VMEM((8, LANES), jnp.int32),
            pltpu.VMEM((3, 8, LANES), jnp.int32),
            pltpu.VMEM((STEPS, len(SIDES), ROWS, LANES), jnp.float32),
            pltpu.VMEM((STEPS, len(SIDES), ROWS, LANES), jnp.float32),
            pltpu.VMEM((len(SHIFTS), 3, ROWS + 2 * HALO, LANES), jnp.float32),
            pltpu.VMEM((len(SHIFTS), ROWS + 2 * HALO, LANES), jnp.float32),
            pltpu.VMEM((len(OFFSETS), ROWS, LANES), jnp.float32),
            pltpu.VMEM((len(OFFSETS), ROWS, LANES), jnp.float32),
            pltpu.VMEM((3, ROWS, LANES), jnp.float32),
            pltpu.VMEM((3, ROWS, LANES), jnp.float32),
            pltpu.VMEM((ROWS, LANES), jnp.float32),
            pltpu.VMEM((ROWS, LANES), jnp.int32),
            pltpu.SemaphoreType.DMA((2, 3)),
            pltpu.SemaphoreType.DMA((STEPS, len(SIDES))),
            pltpu.SemaphoreType.DMA((STEPS, len(SIDES))),
        ],
        compiler_params=pltpu.CompilerParams(collective_id=0, has_side_effects=True),
    )(
        positions.reshape(3, ROWS, LANES),
        velocities.reshape(3, ROWS, LANES),
        bead_types.reshape(ROWS, LANES),
        tiles.reshape(2, -1),
        table,
    )
    return new_pos.reshape(positions.shape), new_vel.reshape(velocities.shape)


def solution(mesh):
    return jax.shard_map(
        functools.partial(per_device, mesh.shape["gx"], mesh.shape["gy"]),
        mesh=mesh,
        in_specs=(
            P(None, "gx", "gy", None),
            P(None, "gx", "gy", None),
            P("gx", "gy", None),
            P(),
            P(),
            P("gx", "gy", None),
            P("gx", "gy", None),
            P("gx", "gy", None, None),
        ),
        out_specs=(P(None, "gx", "gy", None), P(None, "gx", "gy", None)),
        check_vma=False,
    )
```

time: 485 us -> 47.3 us (0.10); the launches traced: 476 us -> 47 us
  local copies, waits for them, and re-layouts: 165 us -> 2.9 us
  matrix products: 143 us -> 0 us
  other arithmetic: 122 us -> 0.67 us
  Pallas kernels: 0 us -> 42.8 us
  starting transfers between devices: 24.4 us -> 0 us
  waiting for transfers between devices: 15.3 us -> 0 us
    dot_general x36 -> x0, matrix products: 143 us -> none  [the longest x28 141 us: pair_block(): jnp.einsum('kni,knj->kij', eps_rows, onehot_b, precision=lax.Precision.HI...]
    gather x186 -> x0, local copies, waits for them, and re-layouts: 117 us -> none  [the longest x28 16.5 us: one_block(): pos_zone[:, right_ids]]
    scatter-add x64 -> x0, other arithmetic: 103 us -> none  [the longest x8 41.1 us: step_forces(): return f_home.at[:, x_index].add(own_x).at[:, y_index].add(own_y)]
    pallas_call x0 -> x1, Pallas kernels: none -> 42.8 us  [per_device(): pl.pallas_call(functools.partial(kernel, n_gx, n_gy, side), out_shape=(sh...]
    ppermute x16 -> x0, starting transfers between devices: 24.4 us -> none  [from_behind(): lax.ppermute(array, axis, [(i, (i + by) % peers) for i in range(peers)])]
    slice x88 -> x0, local copies, waits for them, and re-layouts: 16.9 us -> none  [the longest x4 7.35 us: step_forces(): f_home = forces[:, :beads]]
    ppermute x16 -> x0, waiting for transfers between devices: 15.3 us -> none  [from_behind(): lax.ppermute(array, axis, [(i, (i + by) % peers) for i in range(peers)])]
    add x11 -> x0, other arithmetic: 10.2 us -> none  [the longest x3 6.54 us: per_device(): coords = coords + TIME_STEP * speeds]
  transfers between devices with their start and end apart: 16 -> 0, of which waited for: 11 -> 0; matrix products, arithmetic and copies ran while one was open for 11% -> 0% of each run, Pallas kernels for 0% -> 0%
where the time goes in v1:
time: 47.3 us; the launch traced here: 47 us
  Pallas kernels  42.8 us (90%)
  local copies, waits for them, and re-layouts  2.9 us (6%)
  other arithmetic  0.67 us (1%)
  between operations  0.67 us (1%)
    pallas_call x1, Pallas kernels, per_device(): pl.pallas_call(functools.partial(kernel, n_gx, n_gy, side), out_shape=(sh...  42.8 us
    unnamed x7, local copies, waits for them, and re-layouts  2.06 us

profile of v1, /device:TPU:0, one launch (start us, length us, event | category | flops | bytes accessed | tf_op | source)
XLA Modules:
  0.0 47.0 jit_solution(12576887836702875099)
XLA Ops:
  0.6 0.0 copy-start
  0.6 0.7 %pad_bitcast_fusion.1 = f32[1,128]{1,0:T(1,128)S(1)} fusion(f32[18]{0:T(128)} %param.12), kind=kLoop, calls=%fused_computation.4 | loop fusion | bytes 584 | tf_op jit(solution)/shard_map/broadcast_in_dim | solution.py:370
  1.3 0.1 pad.17.clone
  1.4 0.0 copy-done
  1.4 0.1 copy.11
  1.5 0.1 reshape.32
  1.6 0.7 %maximum_maximum_fusion.table_ref = f32[8,128]{1,0:T(8,128)} fusion(f32[1,128]{1,0:T(1,128)S(1)} %pad_bitcast_fusion.1, f32[3,128]{1,0:T(4,128)S(1)} %pad_bitcast_fusion, f32[8]{0:T(128)S(1)} %pad.17.clone), kind=kLoop, calls=%fused_computation.2 | loop fusion | flops 2048 | bytes 6176 | tf_op jit(solution)/shard_map/concatenate | solution.py:371
  2.3 42.8 %shard_map.77 = (f32[3,16,128]{2,1,0:T(8,128)}, f32[3,16,128]{2,1,0:T(8,128)}) custom-call(f32[3,16,128]{2,1,0:T(8,128)} %bitcast.16, f32[3,16,128]{2,1,0:T(8,128)} %bitcast.17, s32[16,128]{1,0:T(8,128)} %bitcast.18, s32[2,112]{1,0:T(2,128)} %bitcast.19, f32[8,128]{1,0:T(8,128)} %maximum_maximum_fusion.table_ref), custom_call_target="tpu_custom_call" | custom-call | tf_op jit(solution)/shard_map/pallas_call | solution.py:374
  45.1 0.0 copy-start.1
  45.1 1.4 %copy.16 = f32[3,1,1,2048]{3,2,1,0:T(1,128)} copy(f32[3,1,1,2048]{3,2,1,0:T(1,128)} %bitcast.15) | data formatting | bytes 49152
  46.4 0.0 copy-done.1
  46.4 0.6 %copy.17 = f32[3,1,1,2048]{3,2,1,0:T(1,128)} copy(f32[3,1,1,2048]{3,2,1,0:T(1,128)S(1)} %bitcast.14) | data formatting | bytes 49152
  (4 shorter events, 0.0 us)
Async XLA Ops:
  0.6 0.8 %copy-start = (f32[18,18]{1,0:T(8,128)S(1)}, f32[18,18]{1,0:T(8,128)}, u32[]{:S(2)}) copy-start(f32[18,18]{1,0:T(8,128)} %param.11) | copy-start | bytes 3892
  45.1 1.4 %copy-start.1 = (f32[3,16,128]{2,1,0:T(8,128)S(1)}, f32[3,16,128]{2,1,0:T(8,128)}, u32[]{:S(2)}) copy-start(f32[3,16,128]{2,1,0:T(8,128)} %get-tuple-element.5) | copy-start | bytes 73732

commit v2 on v1

--- a/solution.py
+++ b/solution.py
@@ -23,13 +23,26 @@
 NONE = 31
 SIDES = [(-1, -1), (-1, 0), (-1, 1), (0, -1), (0, 1), (1, -1), (1, 0), (1, 1)]
 ZONES = [(0, 0), (1, 0), (0, 1), (1, 1)]
-SHIFTS = [(dx, dy) for dy in range(-2, 3) for dx in range(-2, 3)]
-OFFSETS = [
-    (number, dz)
-    for number, (dx, dy) in enumerate(SHIFTS)
-    for dz in range(-2, 3)
-    if 0 < dx * dx + dy * dy + dz * dz <= 8
+NEAR = [(dx, dy) for dy in range(-2, 3) for dx in range(-2, 3) if 0 < dx * dx + dy * dy <= 4]
+MIDDLE = [(dx, dy) for dy in range(-2, 3) for dx in range(-2, 3) if dx * dx + dy * dy == 5]
+FAR = [(dx, dy) for dy in range(-2, 3) for dx in range(-2, 3) if dx * dx + dy * dy == 8]
+SHIFTS = NEAR + MIDDLE + FAR + [(0, 0)]
+RUNS = [
+    (0, len(NEAR), (-2, -1, 0, 1, 2), 0),
+    (len(NEAR), len(MIDDLE), (-1, 0, 1), 5 * len(NEAR)),
+    (len(NEAR) + len(MIDDLE), len(FAR), (0,), 5 * len(NEAR) + 3 * len(MIDDLE)),
+    (len(SHIFTS) - 1, 1, (-2, -1, 1, 2), 5 * len(NEAR) + 3 * len(MIDDLE) + len(FAR)),
 ]
+COUNT = RUNS[3][3] + 4
+UNIT = SIGMA * 2.0 ** (1.0 / 6.0)
+REACH = (CUTOFF / UNIT) ** 2
+TAPER = (UNIT / CUTOFF) ** 4
+LJ_FACTOR = 12.0 / UNIT**2 * TAPER
+Q_FACTOR = COULOMB / UNIT**3 * TAPER
+Q_SHIFT = (UNIT / CUTOFF) ** 3
+PER_ROW = 6
+STRIDE = 21
+UNROLL = 2
 
 
 def lane_gather(values, index):
@@ -38,9 +51,9 @@
 
 def kernel(
     n_gx, n_gy, side,
-    pos_ref, vel_ref, kind_ref, tile_ref, table_ref,
+    pos_ref, vel_ref, kind_ref, tile_ref, eps_ref, charge_ref,
     out_pos_ref, out_vel_ref,
-    tile_send, tile_recv, send, recv, ext, kind_ext, coef_lj, coef_q, now, speed, mix, site_ref,
+    tile_send, tile_recv, send, recv, ext, kind_ext, charge_ext, coef_lj, coef_q, now, speed, mix, site_ref, square,
     tile_sems, send_sems, recv_sems,
 ):
     width = side * SPACING
@@ -198,7 +211,6 @@
         ref[pl.ds(HALO + ROWS, HALO), :] = pltpu.roll(values[:8], 64, 1)
 
     def gather_images(turn, component, own):
-        shift_of = (width, width, 0.0, 0.0)
         images = {(0, 0): own}
         for ux, uy in SIDES:
             got = image(turn, ux, uy, component)
@@ -218,8 +230,23 @@
     def spread_positions(turn, own):
         for component in range(3):
             images = gather_images(turn, component, own[component])
+            images = {key: value * (1.0 / UNIT) for key, value in images.items()}
             for number, (dx, dy) in enumerate(SHIFTS):
                 put_extended(ext.at[number, component], merge_and_shift(images, dx, dy))
+
+    square[...] = jnp.zeros((LANES, LANES), jnp.float32)
+    square[0:NTYPES, 0:NTYPES] = eps_ref[...]
+    padded = square[...]
+    square[...] = (padded + padded.T) * (0.5 * LJ_FACTOR)
+    eps_rows = []
+    for k in range(NTYPES // PER_ROW):
+        flat = square[PER_ROW * k : PER_ROW * k + 1, :]
+        for m in range(1, PER_ROW):
+            flat = flat + pltpu.roll(square[PER_ROW * k + m : PER_ROW * k + m + 1, :], STRIDE * m, 1)
+        eps_rows.append(jnp.broadcast_to(flat, (ROWS, LANES)))
+    mix[0:1, :] = jnp.zeros((1, LANES), jnp.float32)
+    mix[0:1, 0:NTYPES] = charge_ref[...]
+    charge_row = jnp.broadcast_to(mix[0:1, :], (ROWS, LANES))
 
     pl.semaphore_wait(barrier, len(SIDES))
     own = [now[component] for component in range(3)]
@@ -274,70 +301,87 @@
             table = table + jnp.where(half == 0, picked[0], picked[1])
         tables.append(table)
 
+    cat_x, cat_y = (lane >> 2) & 3, lane & 3
+    weight_of = {}
+    for dz in range(-2, 3):
+        layer = half * ROWS + row + dz
+        in_z = (layer >= 0) & (layer < 2 * ROWS)
+        total = jnp.zeros((ROWS, LANES), jnp.float32)
+        for zone, (ox, oy) in enumerate(ZONES):
+            on_x = (cat_x >= 2) if ox else (cat_x <= 2)
+            on_y = (cat_y >= 2) if oy else (cat_y <= 2)
+            in_x = cat_x == (2 if ox else 1)
+            in_y = cat_y == (2 if oy else 1)
+            start = jnp.where(in_x, jnp.where(in_y, 24, 16), jnp.where(in_y, 20, 0))
+            shift = jnp.where(in_x, jnp.where(in_y, 6, 3), jnp.where(in_y, 3, 1))
+            which = jnp.where(on_x & on_y & in_z, start + (layer >> shift), NONE)
+            total = total + lane_gather(tables[zone >> 1], half * 64 + 32 * (zone & 1) + which)
+        weight_of[dz] = total
+
+    def category(site, step):
+        other = site + step
+        return jnp.where(
+            other >= side, 1, jnp.where(other < 0, 3, jnp.where((site < 2) & (other < 2), 2, 0))
+        )
+
     kind_images = gather_images(0, 3, kind)
-    kind_own = kind.astype(jnp.int32)
-    eps_rows = [jnp.broadcast_to(table_ref[k : k + 1, :], (ROWS, LANES)) for k in range(4)]
-    charge_own = lane_gather(eps_rows[3], kind_own)
+    kind_images = {key: value.astype(jnp.int32) for key, value in kind_images.items()}
+    charge_images = {key: lane_gather(charge_row, value) for key, value in kind_images.items()}
+    kind_own = kind_images[(0, 0)]
+    kind_row = sum((kind_own >= PER_ROW * k).astype(jnp.int32) for k in range(1, 4))
+    kind_base = (kind_own - PER_ROW * kind_row) * STRIDE
+    in_row = [kind_row == k for k in range(3)]
     for number, (dx, dy) in enumerate(SHIFTS):
         put_extended(kind_ext.at[number], merge_and_shift(kind_images, dx, dy))
-
-    zone_of = []
-    for number, (dx, dy) in enumerate(SHIFTS):
-        masks = []
-        for ox, oy in ZONES:
-            px, py = x_site + ox * side, y_site + oy * side
-            qx, qy = px + dx, py + dy
-            limit = side + 2
-            inside = (px < limit) & (py < limit) & (qx >= 0) & (qx < limit) & (qy >= 0) & (qy < limit)
-            in_x, in_y = qx >= side, qy >= side
-            start = jnp.where(in_x, jnp.where(in_y, 24, 16), jnp.where(in_y, 20, 0))
-            shift = jnp.where(in_x, jnp.where(in_y, 6, 3), jnp.where(in_y, 3, 1))
-            masks.append((inside, start, shift))
-        for dz in range(-2, 3):
-            if (number, dz) not in OFFSETS:
-                continue
-            place = OFFSETS.index((number, dz))
-            layer = half * ROWS + row + dz
-            in_z = (layer >= 0) & (layer < 2 * ROWS)
-            weight = jnp.zeros((ROWS, LANES), jnp.float32)
-            for zone in range(4):
-                ox, oy = ZONES[zone]
-                inside, start, shift = masks[zone]
-                which = jnp.where(inside & in_z, start + (layer >> shift), NONE)
-                weight = weight + lane_gather(
-                    tables[zone >> 1], half * 64 + 32 * (zone & 1) + which
-                )
-            other = kind_ext[number, pl.ds(HALO + dz, ROWS), :].astype(jnp.int32)
-            pair = kind_own * (NTYPES + 1) + other
-            low = pair & (LANES - 1)
-            high = pair >> 7
-            depth = jnp.where(
-                high == 0,
-                lane_gather(eps_rows[0], low),
-                jnp.where(high == 1, lane_gather(eps_rows[1], low), lane_gather(eps_rows[2], low)),
-            )
-            coef_lj[place] = weight * depth * (24.0 * SIGMA**6)
-            coef_q[place] = weight * (COULOMB * charge_own) * lane_gather(eps_rows[3], other)
+        put_extended(charge_ext.at[number], merge_and_shift(charge_images, dx, dy))
+    charge_own = charge_images[(0, 0)] * Q_FACTOR
+    for first, length, depths, base in RUNS:
+        for sub in range(length):
+            number = first + sub
+            dx, dy = SHIFTS[number]
+            chosen = half * 64 + category(x_site, dx) * 4 + category(y_site, dy)
+            for turn, dz in enumerate(depths):
+                place = base + sub * len(depths) + turn
+                weight = lane_gather(weight_of[dz], chosen)
+                rows = pl.ds(HALO + dz, ROWS)
+                low = kind_base + kind_ext[number, rows, :]
+                depth = jnp.where(in_row[2], lane_gather(eps_rows[2], low), 0.0)
+                depth = jnp.where(in_row[1], lane_gather(eps_rows[1], low), depth)
+                depth = jnp.where(in_row[0], lane_gather(eps_rows[0], low), depth)
+                coef_lj[place] = weight * depth
+                coef_q[place] = weight * (charge_own * charge_ext[number, rows, :])
+
+    def add_pair(scaled, force, place, number, dz):
+        apart = [scaled[k] - ext[number, k, pl.ds(HALO + dz, ROWS), :] for k in range(3)]
+        dist_sq = apart[0] * apart[0] + apart[1] * apart[1] + apart[2] * apart[2]
+        inv_r = lax.rsqrt(dist_sq)
+        inv_sq = inv_r * inv_r
+        taper = jnp.maximum(REACH - dist_sq, 0.0)
+        inv_4 = inv_sq * inv_sq
+        inv_6 = inv_4 * inv_sq
+        lennard = coef_lj[place] * (inv_4 * inv_4) * (inv_6 - 1.0)
+        coulomb = coef_q[place] * (inv_sq * inv_r - Q_SHIFT)
+        scalar = taper * taper * (lennard + coulomb)
+        return [force[k] + scalar * apart[k] for k in range(3)]
 
     def advance(turn):
         mine = [now[component] for component in range(3)]
         spread_positions(turn, mine)
+        scaled = [mine[k] * (1.0 / UNIT) for k in range(3)]
         force = [jnp.zeros((ROWS, LANES), jnp.float32) for _ in range(3)]
-        for place, (number, dz) in enumerate(OFFSETS):
-            apart = [mine[k] - ext[number, k, pl.ds(HALO + dz, ROWS), :] for k in range(3)]
-            dist_sq = apart[0] * apart[0] + apart[1] * apart[1] + apart[2] * apart[2]
-            inv_r = lax.rsqrt(dist_sq)
-            inv_sq = inv_r * inv_r
-            switch = jnp.maximum(1.0 - dist_sq * (1.0 / (CUTOFF * CUTOFF)), 0.0)
-            inv_4 = inv_sq * inv_sq
-            inv_6 = inv_4 * inv_sq
-            lennard = coef_lj[place] * (inv_4 * inv_4) * (inv_6 * (2.0 * SIGMA**6) - 1.0)
-            coulomb = coef_q[place] * (inv_sq * inv_r - 1.0 / CUTOFF**3)
-            scalar = switch * switch * (lennard + coulomb)
-            for k in range(3):
-                force[k] = force[k] + scalar * apart[k]
+        for first, length, depths, base in RUNS:
+            def run(sub, held):
+                held = list(held)
+                for which, dz in enumerate(depths):
+                    held = add_pair(scaled, held, base + sub * len(depths) + which, first + sub, dz)
+                return tuple(held)
+            if length * len(depths) > 4:
+                force = list(lax.fori_loop(0, length, run, tuple(force), unroll=UNROLL))
+            else:
+                for sub in range(length):
+                    force = list(run(sub, force))
         for k in range(3):
-            new_speed = speed[k] + (TIME_STEP / MASS) * force[k]
+            new_speed = speed[k] + (TIME_STEP / MASS * UNIT) * force[k]
             speed[k] = new_speed
             now[k] = mine[k] + TIME_STEP * new_speed
 
@@ -364,17 +408,12 @@
     beads = positions.shape[-1]
     strip = x_list.shape[-1]
     side = 2 * beads // strip
-    eps_sym = 0.5 * (eps_table + eps_table.T)
-    flat = jnp.pad(eps_sym, ((0, 1), (0, 1))).reshape(-1)
-    flat = jnp.pad(flat, (0, 3 * LANES - flat.shape[0])).reshape(3, LANES)
-    charge_row = jnp.pad(charges, (0, LANES - charges.shape[0]))[None]
-    table = jnp.concatenate([flat, charge_row, jnp.zeros((4, LANES), jnp.float32)], axis=0)
     shape = jax.ShapeDtypeStruct((3, ROWS, LANES), jnp.float32)
     vmem = pl.BlockSpec(memory_space=pltpu.VMEM)
     new_pos, new_vel = pl.pallas_call(
         functools.partial(kernel, n_gx, n_gy, side),
         out_shape=(shape, shape),
-        in_specs=[vmem] * 5,
+        in_specs=[vmem] * 6,
         out_specs=(vmem, vmem),
         scratch_shapes=[
             pltpu.VMEM((8, LANES), jnp.int32),
@@ -382,13 +421,15 @@
             pltpu.VMEM((STEPS, len(SIDES), ROWS, LANES), jnp.float32),
             pltpu.VMEM((STEPS, len(SIDES), ROWS, LANES), jnp.float32),
             pltpu.VMEM((len(SHIFTS), 3, ROWS + 2 * HALO, LANES), jnp.float32),
+            pltpu.VMEM((len(SHIFTS), ROWS + 2 * HALO, LANES), jnp.int32),
             pltpu.VMEM((len(SHIFTS), ROWS + 2 * HALO, LANES), jnp.float32),
-            pltpu.VMEM((len(OFFSETS), ROWS, LANES), jnp.float32),
-            pltpu.VMEM((len(OFFSETS), ROWS, LANES), jnp.float32),
+            pltpu.VMEM((COUNT, ROWS, LANES), jnp.float32),
+            pltpu.VMEM((COUNT, ROWS, LANES), jnp.float32),
             pltpu.VMEM((3, ROWS, LANES), jnp.float32),
             pltpu.VMEM((3, ROWS, LANES), jnp.float32),
             pltpu.VMEM((ROWS, LANES), jnp.float32),
             pltpu.VMEM((ROWS, LANES), jnp.int32),
+            pltpu.VMEM((LANES, LANES), jnp.float32),
             pltpu.SemaphoreType.DMA((2, 3)),
             pltpu.SemaphoreType.DMA((STEPS, len(SIDES))),
             pltpu.SemaphoreType.DMA((STEPS, len(SIDES))),
@@ -399,7 +440,8 @@
         velocities.reshape(3, ROWS, LANES),
         bead_types.reshape(ROWS, LANES),
         tiles.reshape(2, -1),
-        table,
+        eps_table,
+        charges[None],
     )
     return new_pos.reshape(positions.shape), new_vel.reshape(velocities.shape)
 

time: 47.3 us -> 49.3 us (1.042)
  Pallas kernels: 42.8 us -> 46.4 us
  local copies, waits for them, and re-layouts: 2.9 us -> 1.96 us
  other arithmetic: 0.67 us -> 0 us
    pallas_call x1, Pallas kernels: 42.8 us -> 46.4 us  [per_device(): pl.pallas_call(functools.partial(kernel, n_gx, n_gy, side), out_shape=(sh...]
    broadcast_in_dim x2 -> x0, local copies, waits for them, and re-layouts: 0.67 us -> none  [the longest x1 0.66 us: per_device(): charge_row = jnp.pad(charges, (0, LANES - charges.shape[0]))[None]]
    concatenate x1 -> x0, other arithmetic: 0.66 us -> none  [per_device(): jnp.concatenate([flat, charge_row, jnp.zeros((4, LANES), jnp.float32)], a...]
    unnamed x7 -> x4, local copies, waits for them, and re-layouts: 2.06 us -> 1.96 us
where the time goes in v2:
time: 49.3 us; the launch traced here: 49 us
  Pallas kernels  46.4 us (94%)
  local copies, waits for them, and re-layouts  1.96 us (4%)
  between operations  0.65 us (1%)
    pallas_call x1, Pallas kernels, per_device(): pl.pallas_call(functools.partial(kernel, n_gx, n_gy, side), out_shape=(sh...  46.4 us
    unnamed x4, local copies, waits for them, and re-layouts  1.96 us

profile of v2, /device:TPU:0, one launch (start us, length us, event | category | flops | bytes accessed | tf_op | source)
XLA Modules:
  0.0 49.0 jit_solution(14802371387259136955)
XLA Ops:
  0.6 46.4 %shard_map.77 = (f32[3,16,128]{2,1,0:T(8,128)}, f32[3,16,128]{2,1,0:T(8,128)}) custom-call(f32[3,16,128]{2,1,0:T(8,128)} %bitcast.7, f32[3,16,128]{2,1,0:T(8,128)} %bitcast.8, s32[16,128]{1,0:T(8,128)} %bitcast.11, s32[2,112]{1,0:T(2,128)} %bitcast.12, f32[18,18]{1,0:T(8,128)} %eps_ref.1, f32[1,18]{1,0:T(1,128)} %bitcast.13), custom_call_target="tpu_custom_call" | custom-call | tf_op jit(solution)/shard_map/pallas_call | solution.py:413
  47.1 0.0 copy-start
  47.1 1.4 %copy.14 = f32[3,1,1,2048]{3,2,1,0:T(1,128)} copy(f32[3,1,1,2048]{3,2,1,0:T(1,128)} %bitcast.10) | data formatting | bytes 49152
  48.4 0.0 copy-done
  48.4 0.6 %copy.15 = f32[3,1,1,2048]{3,2,1,0:T(1,128)} copy(f32[3,1,1,2048]{3,2,1,0:T(1,128)S(1)} %bitcast.9) | data formatting | bytes 49152
Async XLA Ops:
  47.1 1.4 %copy-start = (f32[3,16,128]{2,1,0:T(8,128)S(1)}, f32[3,16,128]{2,1,0:T(8,128)}, u32[]{:S(2)}) copy-start(f32[3,16,128]{2,1,0:T(8,128)} %get-tuple-element.5) | copy-start | bytes 73732

commit v3 on v2

--- a/solution.py
+++ b/solution.py
@@ -42,7 +42,7 @@
 Q_SHIFT = (UNIT / CUTOFF) ** 3
 PER_ROW = 6
 STRIDE = 21
-UNROLL = 2
+AHEAD = 3
 
 
 def lane_gather(values, index):
@@ -207,8 +207,9 @@
 
     def put_extended(ref, values):
         ref[pl.ds(HALO, ROWS), :] = values
-        ref[pl.ds(0, HALO), :] = pltpu.roll(values[8:], 64, 1)
-        ref[pl.ds(HALO + ROWS, HALO), :] = pltpu.roll(values[:8], 64, 1)
+        turned = pltpu.roll(jnp.where(row8 < 4, values[:8], values[8:]), 64, 1)
+        ref[pl.ds(0, HALO), :] = turned
+        ref[pl.ds(HALO + ROWS, HALO), :] = turned
 
     def gather_images(turn, component, own):
         images = {(0, 0): own}
@@ -227,12 +228,10 @@
         for number in range(len(SIDES)):
             side_copy(turn, number).start()
 
-    def spread_positions(turn, own):
+    def spread_position(images, number):
+        dx, dy = SHIFTS[number]
         for component in range(3):
-            images = gather_images(turn, component, own[component])
-            images = {key: value * (1.0 / UNIT) for key, value in images.items()}
-            for number, (dx, dy) in enumerate(SHIFTS):
-                put_extended(ext.at[number, component], merge_and_shift(images, dx, dy))
+            put_extended(ext.at[number, component], merge_and_shift(images[component], dx, dy))
 
     square[...] = jnp.zeros((LANES, LANES), jnp.float32)
     square[0:NTYPES, 0:NTYPES] = eps_ref[...]
@@ -331,13 +330,19 @@
     kind_row = sum((kind_own >= PER_ROW * k).astype(jnp.int32) for k in range(1, 4))
     kind_base = (kind_own - PER_ROW * kind_row) * STRIDE
     in_row = [kind_row == k for k in range(3)]
-    for number, (dx, dy) in enumerate(SHIFTS):
+    def spread_kind(number):
+        dx, dy = SHIFTS[number]
         put_extended(kind_ext.at[number], merge_and_shift(kind_images, dx, dy))
         put_extended(charge_ext.at[number], merge_and_shift(charge_images, dx, dy))
+
+    for number in range(AHEAD):
+        spread_kind(number)
     charge_own = charge_images[(0, 0)] * Q_FACTOR
     for first, length, depths, base in RUNS:
         for sub in range(length):
             number = first + sub
+            if number + AHEAD < len(SHIFTS):
+                spread_kind(number + AHEAD)
             dx, dy = SHIFTS[number]
             chosen = half * 64 + category(x_site, dx) * 4 + category(y_site, dy)
             for turn, dz in enumerate(depths):
@@ -366,20 +371,21 @@
 
     def advance(turn):
         mine = [now[component] for component in range(3)]
-        spread_positions(turn, mine)
-        scaled = [mine[k] * (1.0 / UNIT) for k in range(3)]
+        images = []
+        for component in range(3):
+            found = gather_images(turn, component, mine[component])
+            images.append({key: value * (1.0 / UNIT) for key, value in found.items()})
+        scaled = [images[k][(0, 0)] for k in range(3)]
         force = [jnp.zeros((ROWS, LANES), jnp.float32) for _ in range(3)]
+        for number in range(AHEAD):
+            spread_position(images, number)
         for first, length, depths, base in RUNS:
-            def run(sub, held):
-                held = list(held)
+            for sub in range(length):
+                number = first + sub
+                if number + AHEAD < len(SHIFTS):
+                    spread_position(images, number + AHEAD)
                 for which, dz in enumerate(depths):
-                    held = add_pair(scaled, held, base + sub * len(depths) + which, first + sub, dz)
-                return tuple(held)
-            if length * len(depths) > 4:
-                force = list(lax.fori_loop(0, length, run, tuple(force), unroll=UNROLL))
-            else:
-                for sub in range(length):
-                    force = list(run(sub, force))
+                    force = add_pair(scaled, force, base + sub * len(depths) + which, number, dz)
         for k in range(3):
             new_speed = speed[k] + (TIME_STEP / MASS * UNIT) * force[k]
             speed[k] = new_speed

time: 49.3 us -> 46.3 us (0.939)
  Pallas kernels: 46.4 us -> 43.5 us
    pallas_call x1, Pallas kernels: 46.4 us -> 43.5 us  [per_device(): pl.pallas_call(functools.partial(kernel, n_gx, n_gy, side), out_shape=(sh...]
where the time goes in v3:
time: 46.3 us; the launch traced here: 46.1 us
  Pallas kernels  43.5 us (94%)
  local copies, waits for them, and re-layouts  1.96 us (4%)
  between operations  0.65 us (1%)
    pallas_call x1, Pallas kernels, per_device(): pl.pallas_call(functools.partial(kernel, n_gx, n_gy, side), out_shape=(sh...  43.5 us
    unnamed x4, local copies, waits for them, and re-layouts  1.96 us

profile of v3, /device:TPU:0, one launch (start us, length us, event | category | flops | bytes accessed | tf_op | source)
XLA Modules:
  0.0 46.1 jit_solution(7919558356268973447)
XLA Ops:
  0.6 43.5 %shard_map.77 = (f32[3,16,128]{2,1,0:T(8,128)}, f32[3,16,128]{2,1,0:T(8,128)}) custom-call(f32[3,16,128]{2,1,0:T(8,128)} %bitcast.7, f32[3,16,128]{2,1,0:T(8,128)} %bitcast.8, s32[16,128]{1,0:T(8,128)} %bitcast.11, s32[2,112]{1,0:T(2,128)} %bitcast.12, f32[18,18]{1,0:T(8,128)} %eps_ref.1, f32[1,18]{1,0:T(1,128)} %bitcast.13), custom_call_target="tpu_custom_call" | custom-call | tf_op jit(solution)/shard_map/pallas_call | solution.py:419
  44.1 0.0 copy-start
  44.1 1.4 %copy.14 = f32[3,1,1,2048]{3,2,1,0:T(1,128)} copy(f32[3,1,1,2048]{3,2,1,0:T(1,128)} %bitcast.10) | data formatting | bytes 49152
  45.5 0.0 copy-done
  45.5 0.6 %copy.15 = f32[3,1,1,2048]{3,2,1,0:T(1,128)} copy(f32[3,1,1,2048]{3,2,1,0:T(1,128)S(1)} %bitcast.9) | data formatting | bytes 49152
Async XLA Ops:
  44.1 1.4 %copy-start = (f32[3,16,128]{2,1,0:T(8,128)S(1)}, f32[3,16,128]{2,1,0:T(8,128)}, u32[]{:S(2)}) copy-start(f32[3,16,128]{2,1,0:T(8,128)} %get-tuple-element.5) | copy-start | bytes 73732

commit v4 on v3

--- a/solution.py
+++ b/solution.py
@@ -40,8 +40,6 @@
 LJ_FACTOR = 12.0 / UNIT**2 * TAPER
 Q_FACTOR = COULOMB / UNIT**3 * TAPER
 Q_SHIFT = (UNIT / CUTOFF) ** 3
-PER_ROW = 6
-STRIDE = 21
 AHEAD = 3
 
 
@@ -53,7 +51,7 @@
     n_gx, n_gy, side,
     pos_ref, vel_ref, kind_ref, tile_ref, eps_ref, charge_ref,
     out_pos_ref, out_vel_ref,
-    tile_send, tile_recv, send, recv, ext, kind_ext, charge_ext, coef_lj, coef_q, now, speed, mix, site_ref, square,
+    tile_send, tile_recv, send, recv, ext, kind_ext, charge_ext, coef_lj, coef_q, now, speed, mix, site_ref, square, eps_own,
     tile_sems, send_sems, recv_sems,
 ):
     width = side * SPACING
@@ -237,12 +235,6 @@
     square[0:NTYPES, 0:NTYPES] = eps_ref[...]
     padded = square[...]
     square[...] = (padded + padded.T) * (0.5 * LJ_FACTOR)
-    eps_rows = []
-    for k in range(NTYPES // PER_ROW):
-        flat = square[PER_ROW * k : PER_ROW * k + 1, :]
-        for m in range(1, PER_ROW):
-            flat = flat + pltpu.roll(square[PER_ROW * k + m : PER_ROW * k + m + 1, :], STRIDE * m, 1)
-        eps_rows.append(jnp.broadcast_to(flat, (ROWS, LANES)))
     mix[0:1, :] = jnp.zeros((1, LANES), jnp.float32)
     mix[0:1, 0:NTYPES] = charge_ref[...]
     charge_row = jnp.broadcast_to(mix[0:1, :], (ROWS, LANES))
@@ -327,9 +319,22 @@
     kind_images = {key: value.astype(jnp.int32) for key, value in kind_images.items()}
     charge_images = {key: lane_gather(charge_row, value) for key, value in kind_images.items()}
     kind_own = kind_images[(0, 0)]
-    kind_row = sum((kind_own >= PER_ROW * k).astype(jnp.int32) for k in range(1, 4))
-    kind_base = (kind_own - PER_ROW * kind_row) * STRIDE
-    in_row = [kind_row == k for k in range(3)]
+    for k in range(NTYPES):
+        row_k = jnp.broadcast_to(square[k : k + 1, :], (ROWS, LANES))
+        eps_own[k] = lane_gather(row_k, kind_own)
+
+    def depth_of(other):
+        level = [eps_own[k] for k in range(NTYPES)] + [jnp.zeros((ROWS, LANES), jnp.float32)]
+        bit = 1
+        while len(level) > 1:
+            odd = (other & bit) != 0
+            joined = [jnp.where(odd, level[k + 1], level[k]) for k in range(0, len(level) - 1, 2)]
+            if len(level) % 2:
+                joined.append(level[-1])
+            level = joined
+            bit = 2 * bit
+        return level[0]
+
     def spread_kind(number):
         dx, dy = SHIFTS[number]
         put_extended(kind_ext.at[number], merge_and_shift(kind_images, dx, dy))
@@ -349,10 +354,7 @@
                 place = base + sub * len(depths) + turn
                 weight = lane_gather(weight_of[dz], chosen)
                 rows = pl.ds(HALO + dz, ROWS)
-                low = kind_base + kind_ext[number, rows, :]
-                depth = jnp.where(in_row[2], lane_gather(eps_rows[2], low), 0.0)
-                depth = jnp.where(in_row[1], lane_gather(eps_rows[1], low), depth)
-                depth = jnp.where(in_row[0], lane_gather(eps_rows[0], low), depth)
+                depth = depth_of(kind_ext[number, rows, :])
                 coef_lj[place] = weight * depth
                 coef_q[place] = weight * (charge_own * charge_ext[number, rows, :])
 
@@ -436,6 +438,7 @@
             pltpu.VMEM((ROWS, LANES), jnp.float32),
             pltpu.VMEM((ROWS, LANES), jnp.int32),
             pltpu.VMEM((LANES, LANES), jnp.float32),
+            pltpu.VMEM((NTYPES, ROWS, LANES), jnp.float32),
             pltpu.SemaphoreType.DMA((2, 3)),
             pltpu.SemaphoreType.DMA((STEPS, len(SIDES))),
             pltpu.SemaphoreType.DMA((STEPS, len(SIDES))),

time: 46.3 us -> 44.6 us (0.963)
  Pallas kernels: 43.5 us -> 41.8 us
    pallas_call x1, Pallas kernels: 43.5 us -> 41.8 us  [per_device(): pl.pallas_call(functools.partial(kernel, n_gx, n_gy, side), out_shape=(sh...]
where the time goes in v4:
time: 44.6 us; the launch traced here: 44.4 us
  Pallas kernels  41.8 us (94%)
  local copies, waits for them, and re-layouts  1.96 us (4%)
  between operations  0.65 us (1%)
    pallas_call x1, Pallas kernels, per_device(): pl.pallas_call(functools.partial(kernel, n_gx, n_gy, side), out_shape=(sh...  41.8 us
    unnamed x4, local copies, waits for them, and re-layouts  1.96 us

profile of v4, /device:TPU:0, one launch (start us, length us, event | category | flops | bytes accessed | tf_op | source)
XLA Modules:
  0.0 44.4 jit_solution(16747759346903183550)
XLA Ops:
  0.6 41.8 %shard_map.77 = (f32[3,16,128]{2,1,0:T(8,128)}, f32[3,16,128]{2,1,0:T(8,128)}) custom-call(f32[3,16,128]{2,1,0:T(8,128)} %bitcast.7, f32[3,16,128]{2,1,0:T(8,128)} %bitcast.8, s32[16,128]{1,0:T(8,128)} %bitcast.11, s32[2,112]{1,0:T(2,128)} %bitcast.12, f32[18,18]{1,0:T(8,128)} %eps_ref.1, f32[1,18]{1,0:T(1,128)} %bitcast.13), custom_call_target="tpu_custom_call" | custom-call | tf_op jit(solution)/shard_map/pallas_call | solution.py:421
  42.4 0.0 copy-start
  42.4 1.4 %copy.14 = f32[3,1,1,2048]{3,2,1,0:T(1,128)} copy(f32[3,1,1,2048]{3,2,1,0:T(1,128)} %bitcast.10) | data formatting | bytes 49152
  43.8 0.0 copy-done
  43.8 0.6 %copy.15 = f32[3,1,1,2048]{3,2,1,0:T(1,128)} copy(f32[3,1,1,2048]{3,2,1,0:T(1,128)S(1)} %bitcast.9) | data formatting | bytes 49152
Async XLA Ops:
  42.4 1.4 %copy-start = (f32[3,16,128]{2,1,0:T(8,128)S(1)}, f32[3,16,128]{2,1,0:T(8,128)}, u32[]{:S(2)}) copy-start(f32[3,16,128]{2,1,0:T(8,128)} %get-tuple-element.5) | copy-start | bytes 73732
